TPU v7x, 128 devices: a whole 4x4x4 slice. The times are simulated.
128 devices in a mesh: row: 16 (over x, y_hi, core), col: 8 (over z, y_lo).
Axes of the slice: x: 4, y: 4 (y_hi: 2, y_lo: 2; y = y_hi * 2 + y_lo), z: 4, core: 2. Of those that a mesh axis runs over, the one named last changes fastest.
Arguments:
- object_field: float32 [2, 8192, 4096], P(None, 'row', 'col'), may hold values from -6 to 6
- probe: float32 [3, 2, 256, 256], replicated, may hold values from -6 to 6
- raw_counts: bfloat16 [768, 256, 256], P(('row', 'col')), may hold values from 0.099609375 to 10
- resample_delta: float32 [256, 256], replicated, may hold values from -0.1875 to 0.1875
- tile_row: int32 [768, 1], P(('row', 'col')), may hold values from 0 to 15; in each aligned block of 6 rows (0 to 5, 6 to 11, ...) no two rows name the same one
- offsets: int32 [768, 2], P(('row', 'col')), may hold values from 0 to 511
Outputs:
- object_grad: float32 [2, 8192, 4096], P(None, 'row', 'col')
- probe_grad: float32 [3, 2, 256, 256], replicated
Inputs may be any that keep to these rules, and one draw needn't show every extreme that they name: `tile_row`: the 6 frames of one device have distinct tile rows.
All inputs are finite; a program needn't handle non-finite values.
Results may differ from a plain program's by a relative error of at most 0.0008.
The roundings to bfloat16 on the way count: a program that leaves them out, or rounds other values in their place, can miss the bound.
Values may be sent and summed in bfloat16 or wider, within the bound.
No kernel may reach another device: no remote copies, remote signals or barrier semaphores. Data moves between devices by JAX's collectives and lax.ppermute only.
A program may use at most 128 MiB of HBM per device.

v0:
```python
import math

import jax
import jax.numpy as jnp
from jax import lax
from jax.sharding import Mesh
from jax.sharding import PartitionSpec as P

ROW = ("row_0", "row_1", "row_2")
ROW_COL = ("row_0", "row_1", "row_2", "col")


def extended_2(value, sides, width):
    for axis, dim in sides:
        size, length = (lax.axis_size(axis), value.shape[dim])
        up = [(i, (i + 1) % size) for i in range(size - 1)]
        down = [(j, i) for i, j in up]
        last = lax.slice_in_dim(value, length - width, length, axis=dim)
        first = lax.slice_in_dim(value, 0, width, axis=dim)
        before = lax.ppermute(last, axis, up)
        after = lax.ppermute(first, axis, down)
        value = jnp.concatenate([before, value, after], axis=dim)
    return value


def cut_along(value, dim, size):
    before, after = (value.shape[:dim], value.shape[dim + 1 :])
    return jnp.moveaxis(value.reshape(*before, size, -1, *after), dim, 0)


def laid_out(pieces, dim):
    shape = list(pieces.shape[1:])
    shape[dim] *= pieces.shape[0]
    return jnp.moveaxis(pieces, 0, dim).reshape(shape)


def exchange_in_order(pieces, axes, sequence):
    shape = [lax.axis_size(a) for a in axes]
    pieces = pieces.reshape(*shape, *pieces.shape[1:])
    for k in sequence:
        pieces = lax.all_to_all(pieces, axes[k], split_axis=k, concat_axis=k, tiled=True)
    return pieces.reshape(-1, *pieces.shape[len(axes) :])


def two_step_exchange(value, groups, sequence, split_dim, concat_dim):
    size = lax.axis_size(groups[0]) * lax.axis_size(groups[1])
    pieces = cut_along(value, split_dim, size)
    return laid_out(exchange_in_order(pieces, groups, sequence), concat_dim)


def product(left, right):
    return jnp.dot(left, right, preferred_element_type=jnp.float32)


def dft_tables(points):
    indices = jnp.arange(points, dtype=jnp.int32)
    phases = indices[:, None] * indices[None, :] % points
    angles = phases.astype(jnp.float32) * (2.0 * math.pi / points)
    norming = 1.0 / math.sqrt(points)
    cosine = jnp.cos(angles) * norming
    sine_part = -jnp.sin(angles) * norming
    forward = jnp.concatenate(
        [jnp.concatenate([cosine, -sine_part], 1), jnp.concatenate([sine_part, cosine], 1)], 0
    )
    backward = jnp.concatenate(
        [jnp.concatenate([cosine, sine_part], 1), jnp.concatenate([-sine_part, cosine], 1)], 0
    )
    return (forward.astype(jnp.bfloat16), backward.astype(jnp.bfloat16))


def measure(raw_counts, resample_delta):
    points = resample_delta.shape[0]
    resample = (jnp.eye(points, dtype=jnp.float32) + resample_delta).astype(jnp.bfloat16)
    first = jnp.einsum(
        "ij,kjl->kil", resample, raw_counts, preferred_element_type=jnp.float32
    ).astype(jnp.bfloat16)
    second = jnp.einsum("kij,lj->kil", first, resample, preferred_element_type=jnp.float32)
    return jnp.sqrt(jnp.maximum(second, 0.0)).astype(jnp.bfloat16)


def frame_terms(window, probe, amplitude, forward, backward):
    mode_count = probe.shape[0]
    points = probe.shape[-1]
    probe_real = probe[:, 0]
    probe_imag = probe[:, 1]
    object_real = window[0]
    object_imag = window[1]
    wave = jnp.stack(
        [
            probe_real * object_real - probe_imag * object_imag,
            probe_real * object_imag + probe_imag * object_real,
        ],
        1,
    )
    wave_cols = (
        wave.transpose(1, 2, 0, 3).reshape(2 * points, mode_count * points).astype(jnp.bfloat16)
    )
    half_done = product(forward, wave_cols).astype(jnp.bfloat16)
    wave_rows = (
        half_done.reshape(2, points, mode_count, points)
        .transpose(2, 1, 0, 3)
        .reshape(mode_count * points, 2 * points)
    )
    far_field = product(wave_rows, backward).reshape(mode_count, points, 2, points)
    intensity = jnp.sum(far_field * far_field, axis=(0, 2))
    scaling = 1.0 - amplitude.astype(jnp.float32) / jnp.sqrt(jnp.maximum(intensity, 1.0))
    residual = (
        (far_field * scaling[None, :, None, :])
        .astype(jnp.bfloat16)
        .reshape(mode_count * points, 2 * points)
    )
    back_rows = product(residual, forward).astype(jnp.bfloat16)
    back_cols = (
        back_rows.reshape(mode_count, points, 2, points)
        .transpose(2, 1, 0, 3)
        .reshape(2 * points, mode_count * points)
    )
    update = (
        product(backward, back_cols).reshape(2, points, mode_count, points).transpose(2, 0, 1, 3)
    )
    update_real = update[:, 0]
    update_imag = update[:, 1]
    object_term = jnp.stack(
        [
            jnp.sum(probe_real * update_real + probe_imag * update_imag, 0),
            jnp.sum(probe_real * update_imag - probe_imag * update_real, 0),
        ],
        0,
    )
    probe_term = jnp.stack(
        [
            object_real * update_real + object_imag * update_imag,
            object_real * update_imag - object_imag * update_real,
        ],
        1,
    )
    return (object_term, probe_term)


def place(gradient, term, top, left):
    anchor = jnp.zeros((), jnp.int32)
    current = lax.dynamic_slice(gradient, (anchor, top, left), term.shape)
    return lax.dynamic_update_slice(gradient, current + term, (anchor, top, left))


def fold(folded, width, tile):
    pieces = ((0, width, 0), (2 * width, tile, 0), (tile + 3 * width, width, tile - width))
    result = jnp.zeros((folded.shape[0], tile, tile), jnp.float32)
    for source_row, length_row, target_row in pieces:
        for source_col, length_col, target_col in pieces:
            block = folded[
                :, source_row : source_row + length_row, source_col : source_col + length_col
            ]
            result = result.at[
                :, target_row : target_row + length_row, target_col : target_col + length_col
            ].add(block)
    return result


def shards(object_field, probe, raw_counts, resample_delta, tile_row, offsets):
    points = probe.shape[-1]
    half = points // 2
    tile = object_field.shape[1]
    tile_rows = lax.axis_size(ROW)
    frame_total = raw_counts.shape[0] * tile_rows * lax.axis_size("col")
    forward, backward = dft_tables(points)
    amplitudes = measure(raw_counts, resample_delta)
    extended = extended_2(object_field, ((ROW, 1), ("col", 2)), half)
    slot_ids = jnp.arange(tile_rows, dtype=jnp.int32)
    target = tile_row[:, 0]
    picks = (target[:, None] == slot_ids[None, :]).astype(jnp.int32)
    live = jnp.sum(picks, 0)
    slot_tops = jnp.sum(picks * offsets[:, 0:1], 0)
    slot_lefts = jnp.sum(picks * offsets[:, 1:2], 0)
    requests = jnp.stack([slot_tops, slot_lefts, live], 1)
    zero_grad = jnp.zeros(extended.shape, jnp.float32)
    zero_probe = jnp.zeros(probe.shape, jnp.float32)
    anchor = jnp.zeros((), jnp.int32)
    received = two_step_exchange(requests, (("row_0", "row_1"), "row_2"), (1, 0), 0, 0)

    def cut_window(request):
        return lax.dynamic_slice(extended, (anchor, request[0], request[1]), (2, points, points))

    windows = jax.vmap(cut_window)(received)
    returned = lax.all_to_all(windows, ROW, split_axis=0, concat_axis=0, tiled=True)
    own_windows = returned[target]

    def one_frame(probe_total, inputs):
        amplitude, window = inputs
        object_term, probe_term = frame_terms(window, probe, amplitude, forward, backward)
        return (probe_total + probe_term, object_term)

    probe_total, terms = lax.scan(one_frame, zero_probe, (amplitudes, own_windows))
    outgoing = jnp.zeros((tile_rows,) + terms.shape[1:], jnp.float32).at[target].set(terms)
    arrived = lax.all_to_all(outgoing, ROW, split_axis=0, concat_axis=0, tiled=True)

    def add_slot(slot, gradient):
        request = received[slot]
        return place(gradient, arrived[slot], request[0], request[1])

    gradient = lax.fori_loop(0, tile_rows, add_slot, zero_grad)
    probe_grad = lax.psum(probe_total, ROW_COL) * (1.0 / math.sqrt(frame_total))
    folded = extended_2(gradient, ((ROW, 1), ("col", 2)), half)
    object_grad = fold(folded, half, tile)
    return (object_grad, probe_grad)


def solution(mesh):
    torus = Mesh(
        mesh.devices.reshape(4, 2, 2, mesh.shape["col"]), ("row_0", "row_1", "row_2", "col")
    )
    return jax.shard_map(
        shards,
        mesh=torus,
        in_specs=(
            P(None, ROW, "col"),
            P(),
            P(ROW_COL, None, None),
            P(),
            P(ROW_COL, None),
            P(ROW_COL, None),
        ),
        out_specs=(P(None, ROW, "col"), P()),
        check_vma=False,
    )
```

profile of v0, /device:TPU:1, one launch (start us, length us, event | category | flops | bytes accessed | tf_op | source)
XLA Modules:
  0.0 1067.9 jit_solution(17176827742125232952)
XLA Ops:
  16.8 10.9 %collective-permute-done = f32[2,128,512]{2,1,0:T(8,128)S(1)} collective-permute-done((f32[2,128,512]{2,1,0:T(8,128)S(1)}, f32[2,128,512]{2,1,0:T(8,128)S(1)}, u32[]{:S(2)}, u32[]{:S(2)}) %collective-permute-start) | collective-permute-done | bytes 524320 | tf_op jit(solution)/shard_map/ppermute | solution.py:20
  37.7 9.1 all-to-all-start.1
  53.5 7.9 collective-permute-done.3
  70.0 65.0 %while.38 = (s32[]{:T(128)}, f32[2,768,768]{2,1,0:T(8,128)}, s32[16,3]{0,1:T(4,128)S(1)}, f32[16,2,256,256]{3,2,1,0:T(8,128)}, s32[]{:T(128)}) while((s32[]{:T(128)}, f32[2,768,768]{2,1,0:T(8,128)}, s32[16,3]{0,1:T(4,128)S(1)}, f32[16,2,256,256]{3,2,1,0:T(8,128)}, s32[]{:T(128)}) %tuple.136), condition=%wide.while_cond.9, body=%wide.while_body.9.sunk | while | flops 2 | bytes 1050217 | solution.py:182
  135.0 14.1 %all-to-all-start.2 = ((f32[16,2,256,256]{3,2,1,0:T(8,128)}), f32[16,2,256,256]{3,2,1,0:T(8,128)}, u32[]{:S(2)}, u32[]{:S(2)}) async-start(f32[16,2,256,256]{3,2,1,0:T(8,128)} %get-tuple-element.250), calls=%async_computation.2 | async-start | bytes 16777216 | tf_op jit(solution)/shard_map/all_to_all | solution.py:185
  157.5 123.1 %all-to-all-done.2 = f32[16,2,256,256]{3,2,1,0:T(8,128)} async-done(((f32[16,2,256,256]{3,2,1,0:T(8,128)}), f32[16,2,256,256]{3,2,1,0:T(8,128)}, u32[]{:S(2)}, u32[]{:S(2)}) %all-to-all-start.2) | async-done | bytes 8388640 | tf_op jit(solution)/shard_map/all_to_all | solution.py:185
  286.5 245.4 %while.39 = (s32[]{:T(128)}, f32[3,2,256,256]{2,1,3,0:T(2,128)}, f32[6,2,256,256]{3,2,1,0:T(8,128)}, f32[6,2,256,256]{3,2,1,0:T(8,128)}, f32[3,2,256,256]{2,1,3,...) while((s32[]{:T(128)}, f32[3,2,256,256]{2,1,3,0:T(2,128)}, ...), condition=%wide.region_7.8_spmd.clone, body=%wide.region_3.7_spmd.clone.sunk | while | flops 1620246528 | bytes 56230624 | solution.py:193
  310.3 8.3 add_reduce_fusion.2
  350.0 8.3 add_reduce_fusion.2
  391.1 8.3 add_reduce_fusion.2
  432.3 8.3 add_reduce_fusion.2
  473.4 8.3 add_reduce_fusion.2
  514.5 8.3 add_reduce_fusion.2
  536.1 7.2 scatter_fusion
  543.3 9.0 all-to-all-start.3
  552.4 131.4 %all-to-all-done.3 = f32[16,2,256,256]{3,2,1,0:T(8,128)} async-done(((f32[16,2,256,256]{3,2,1,0:T(8,128)}), f32[16,2,256,256]{3,2,1,0:T(8,128)}, u32[]{:S(2)}, u32[]{:S(2)}) %all-to-all-start.3) | async-done | bytes 8388640 | tf_op jit(solution)/shard_map/all_to_all | solution.py:195
  686.3 186.0 %while.37 = (s32[]{:T(128)}, f32[2,768,768]{2,1,0:T(8,128)}, s32[16,3]{0,1:T(4,128)S(1)}, f32[16,2,256,256]{3,2,1,0:T(8,128)}, s32[]{:T(128)}, /*index=5*/s32[]{:T(128)}, s32[]{:T(128)}) while((s32[]{:T(128)}, f32[2,768,768]{2,1,0:T(8,128)}, s32[16,3]{0,1:T(4,128)S(1)}, f32[16,2,256,256]{3,2,1,0:T(8,128)}, s32[]{:T(128)}, ...), condition=%wide.region_10.11_spmd, body=%wide.region_9.10_spmd.sunk | while | flops 131080 | bytes 2621645 | solution.py:201
  726.0 6.6 dynamic_update_slice.15
  738.0 6.6 dynamic_update_slice.15
  772.8 6.8 dynamic_update_slice.15
  830.6 6.6 dynamic_update_slice.15
  854.1 6.8 dynamic_update_slice.15
  881.6 13.7 %collective-permute-done.4 = f32[2,128,768]{2,1,0:T(8,128)S(1)} collective-permute-done((f32[2,128,768]{2,1,0:T(8,128)}, f32[2,128,768]{2,1,0:T(8,128)S(1)}, u32[]{:S(2)}, u32[]{:S(2)}) %collective-permute-start.4) | collective-permute-done | bytes 786464 | tf_op jit(solution)/shard_map/ppermute | solution.py:20
  903.6 140.3 %all-reduce.3.cloned.1.call-done = f32[3,2,256,256]{3,2,1,0:T(8,128)} async-done(((f32[3,2,256,256]{3,2,1,0:T(8,128)}), f32[3,2,256,256]{3,2,1,0:T(8,128)}) %all-reduce.3.cloned.1.call-update) | async-done | bytes 1572880 | tf_op jit(solution)/shard_map/psum | solution.py:202
  (390 shorter events, 448.8 us)
Async XLA Ops:
  7.2 148.6 %copy-start = (bf16[6,256,256]{2,1,0:T(8,128)(2,1)S(1)}, bf16[6,256,256]{2,1,0:T(8,128)(2,1)}, u32[]{:S(2)}) copy-start(bf16[6,256,256]{2,1,0:T(8,128)(2,1)} %param.32) | copy-start | bytes 2359300
  7.2 20.5 %copy-start.6 = (f32[2,512,512]{2,1,0:T(8,128)S(1)}, f32[2,512,512]{2,1,0:T(8,128)}, u32[]{:S(2)}) copy-start(f32[2,512,512]{2,1,0:T(8,128)} %param.30) | copy-start | bytes 6291460
  8.6 19.0 %collective-permute-start = (f32[2,128,512]{2,1,0:T(8,128)S(1)}, f32[2,128,512]{2,1,0:T(8,128)S(1)}, u32[]{:S(2)}, u32[]{:S(2)}) collective-permute-start(f32[2,128,512]{2,1,0:T(8,128)S(1)} %get-tuple-element.376), channel_id=1, source_target_pairs={{0,8},{8,16},{16,24},{24,32},{32,40},{40,48},{48,56},{56,64},{64,7... | collective-permute-start | bytes 1572872 | tf_op jit(solution)/shard_map/ppermute | solution.py:20
  14.8 13.1 %collective-permute-start.1 = (f32[2,128,512]{2,1,0:T(8,128)S(1)}, f32[2,128,512]{2,1,0:T(8,128)S(1)}, u32[]{:S(2)}, u32[]{:S(2)}) collective-permute-start(f32[2,128,512]{2,1,0:T(8,128)S(1)} %get-tuple-element.375), channel_id=1, source_target_pairs={{8,0},{16,8},{24,16},{32,24},{40,32},{48,40},{56,48},{64,56},{72,6... | collective-permute-start | bytes 1572872 | tf_op jit(solution)/shard_map/ppermute | solution.py:21
  27.9 5.3 copy-start.12
  27.9 5.4 copy-start.13
  30.6 22.9 %collective-permute-start.2 = (f32[2,768,128]{2,1,0:T(8,128)}, f32[2,768,128]{2,1,0:T(8,128)S(1)}, u32[]{:S(2)}, u32[]{:S(2)}) collective-permute-start(f32[2,768,128]{2,1,0:T(8,128)} %get-tuple-element.373), channel_id=1, source_target_pairs={{0,1},{1,2},{2,3},{3,4},{4,5},{5,6},{6,7},{8,9},{9,10},{10,11},{11... | collective-permute-start | bytes 2359304 | tf_op jit(solution)/shard_map/ppermute | solution.py:20
  31.9 29.5 %collective-permute-start.3 = (f32[2,768,128]{2,1,0:T(8,128)S(1)}, f32[2,768,128]{2,1,0:T(8,128)S(1)}, u32[]{:S(2)}, u32[]{:S(2)}) collective-permute-start(f32[2,768,128]{2,1,0:T(8,128)S(1)} %get-tuple-element.374), channel_id=1, source_target_pairs={{1,0},{2,1},{3,2},{4,3},{5,4},{6,5},{7,6},{9,8},{10,9},{11,10},{12... | collective-permute-start | bytes 2359304 | tf_op jit(solution)/shard_map/ppermute | solution.py:21
  37.7 15.7 %all-to-all-start.1 = ((s32[8,2,1,3]{3,1,2,0:T(2,128)}), s32[8,2,1,3]{3,1,2,0:T(2,128)S(1)}, u32[]{:S(2)}, u32[]{:S(2)}) async-start(s32[8,2,1,3]{3,1,2,0:T(2,128)} %copy.50), calls=%async_computation.1 | async-start | bytes 16384 | tf_op jit(solution)/shard_map/all_to_all | solution.py:41
  135.0 145.6 %all-to-all-start.2 = ((f32[16,2,256,256]{3,2,1,0:T(8,128)}), f32[16,2,256,256]{3,2,1,0:T(8,128)}, u32[]{:S(2)}, u32[]{:S(2)}) async-start(f32[16,2,256,256]{3,2,1,0:T(8,128)} %get-tuple-element.250), calls=%async_computation.2 | async-start | bytes 16777216 | tf_op jit(solution)/shard_map/all_to_all | solution.py:185
  287.8 7.8 copy-start.2
  327.5 7.8 copy-start.2
  368.7 7.8 copy-start.2
  409.8 7.8 copy-start.2
  451.0 7.8 copy-start.2
  492.1 7.8 copy-start.2
  543.3 140.5 %all-to-all-start.3 = ((f32[16,2,256,256]{3,2,1,0:T(8,128)}), f32[16,2,256,256]{3,2,1,0:T(8,128)}, u32[]{:S(2)}, u32[]{:S(2)}) async-start(f32[16,2,256,256]{3,2,1,0:T(8,128)} %scatter_fusion), calls=%async_computation.3 | async-start | bytes 16777216 | tf_op jit(solution)/shard_map/all_to_all | solution.py:195
  552.3 491.5 %all-reduce.3.cloned.1.call-start = ((), (), s32[]{:S(2)}) async-start(), calls=%async_computation.4 | async-start | bytes 3145728 | tf_op jit(solution)/shard_map/psum | solution.py:202
  872.4 7.2 copy-start.3
  875.1 20.2 %collective-permute-start.4 = (f32[2,128,768]{2,1,0:T(8,128)}, f32[2,128,768]{2,1,0:T(8,128)S(1)}, u32[]{:S(2)}, u32[]{:S(2)}) collective-permute-start(f32[2,128,768]{2,1,0:T(8,128)} %get-tuple-element.372), channel_id=1, source_target_pairs={{0,8},{8,16},{16,24},{24,32},{32,40},{40,48},{48,56},{56,64},{64,7... | collective-permute-start | bytes 2359304 | tf_op jit(solution)/shard_map/ppermute | solution.py:20
  877.1 21.4 %collective-permute-start.5 = (f32[2,128,768]{2,1,0:T(8,128)}, f32[2,128,768]{2,1,0:T(8,128)S(1)}, u32[]{:S(2)}, u32[]{:S(2)}) collective-permute-start(f32[2,128,768]{2,1,0:T(8,128)} %get-tuple-element.371), channel_id=1, source_target_pairs={{8,0},{16,8},{24,16},{32,24},{40,32},{48,40},{56,48},{64,56},{72,6... | collective-permute-start | bytes 2359304 | tf_op jit(solution)/shard_map/ppermute | solution.py:21
  899.7 147.0 %collective-permute-start.6 = (f32[2,1024,128]{2,1,0:T(8,128)S(1)}, f32[2,1024,128]{2,1,0:T(8,128)S(1)}, u32[]{:S(2)}, u32[]{:S(2)}) collective-permute-start(f32[2,1024,128]{2,1,0:T(8,128)S(1)} %get-tuple-element.370), channel_id=1, source_target_pairs={{0,1},{1,2},{2,3},{3,4},{4,5},{5,6},{6,7},{8,9},{9,10},{10,11},{11... | collective-permute-start | bytes 3145736 | tf_op jit(solution)/shard_map/ppermute | solution.py:20
  901.0 147.0 %collective-permute-start.7 = (f32[2,1024,128]{2,1,0:T(8,128)}, f32[2,1024,128]{2,1,0:T(8,128)}, u32[]{:S(2)}, u32[]{:S(2)}) collective-permute-start(f32[2,1024,128]{2,1,0:T(8,128)} %get-tuple-element.369), channel_id=1, source_target_pairs={{1,0},{2,1},{3,2},{4,3},{5,4},{6,5},{7,6},{9,8},{10,9},{11,10},{12... | collective-permute-start | bytes 3145736 | tf_op jit(solution)/shard_map/ppermute | solution.py:21
  1056.5 4.6 copy-start.1
  (19 other events, 37.4 us)
Sparse Core Ops, SparseCore 0:
  881.8 162.0 all-reduce.2
where the time goes:
time: 1080 us; the launch traced here: 1070 us
  waiting for transfers between devices  434 us (40%)
  local copies, waits for them, and re-layouts  317 us (29%)
  other arithmetic  154 us (14%)
  loops' own time  54.8 us (5%)
  starting transfers between devices  50.1 us (5%)
  matrix products  40.6 us (4%)
  between operations  14.4 us (1%)
    psum x1, waiting for transfers between devices, shards(): probe_grad = lax.psum(probe_total, ROW_COL) * (1.0 / math.sqrt(frame_total))  140 us
    all_to_all x1, waiting for transfers between devices, shards(): lax.all_to_all(outgoing, ROW, split_axis=0, concat_axis=0, tiled=True)  131 us
    all_to_all x1, waiting for transfers between devices, shards(): lax.all_to_all(windows, ROW, split_axis=0, concat_axis=0, tiled=True)  123 us
    dynamic_update_slice x16, local copies, waits for them, and re-layouts, place(): lax.dynamic_update_slice(gradient, current + term, (anchor, top, left))  98.6 us
    gather x48, local copies, waits for them, and re-layouts  65 us
    another operation x1, loops' own time, shards(): gradient = lax.fori_loop(0, tile_rows, add_slot, zero_grad)  53.7 us
    reduce_sum x6, other arithmetic, frame_terms(): jnp.sum(probe_real * update_real + probe_imag * update_imag, 0)  49.8 us
    dot_general x24, matrix products, product(): return jnp.dot(left, right, preferred_element_type=jnp.float32)  38.9 us
  transfers between devices with their start and end apart: 12, of which 7 were waited for; matrix products, arithmetic and copies ran while one was open for 2% of the time, Pallas kernels for 0%

commit v1 on v0

v1 whole, which is shorter than its diff:
```python
import functools
import math

import jax
import jax.numpy as jnp
from jax import lax
from jax.experimental import pallas as pl
from jax.experimental.pallas import tpu as pltpu
from jax.sharding import Mesh
from jax.sharding import PartitionSpec as P

ROW = ("row_0", "row_1", "row_2")
ROW_COL = ("row_0", "row_1", "row_2", "col")
AROUND = ((-1, -1), (-1, 0), (-1, 1), (0, -1), (0, 1), (1, -1), (1, 0), (1, 1))
VMEM_BYTES = 56 * 2**20


def dft_tables(points):
    indices = jnp.arange(points, dtype=jnp.int32)
    phases = indices[:, None] * indices[None, :] % points
    angles = phases.astype(jnp.float32) * (2.0 * math.pi / points)
    norming = 1.0 / math.sqrt(points)
    cosine = jnp.cos(angles) * norming
    sine_part = -jnp.sin(angles) * norming
    forward = jnp.concatenate(
        [jnp.concatenate([cosine, -sine_part], 1), jnp.concatenate([sine_part, cosine], 1)], 0
    )
    backward = jnp.concatenate(
        [jnp.concatenate([cosine, sine_part], 1), jnp.concatenate([-sine_part, cosine], 1)], 0
    )
    return (forward.astype(jnp.bfloat16), backward.astype(jnp.bfloat16))


def spread_kernel(target, counts, slots, sems):
    copies = [
        pltpu.make_async_copy(counts.at[j], slots.at[target[j]], sems.at[j]) for j in range(counts.shape[0])
    ]
    for copy in copies:
        copy.start()
    for copy in copies:
        copy.wait()


def spread(target, counts, slot_count):
    return pl.pallas_call(
        spread_kernel,
        grid_spec=pltpu.PrefetchScalarGridSpec(
            num_scalar_prefetch=1,
            grid=(1,),
            in_specs=[pl.BlockSpec(memory_space=pl.ANY)],
            out_specs=pl.BlockSpec(memory_space=pl.ANY),
            scratch_shapes=[pltpu.SemaphoreType.DMA((counts.shape[0],))],
        ),
        out_shape=jax.ShapeDtypeStruct((slot_count,) + counts.shape[1:], counts.dtype),
        name="spread",
    )(target, counts)


def regions(half, tile):
    span = {-1: (0, half), 0: (half, tile), 1: (half + tile, half)}
    return [span[a] + span[b] for a, b in ((0, 0),) + AROUND]


def frames_kernel(order, count, tops, lefts, raw, probe, fwd, bwd, res, res_t, *refs, points, modes, spots):
    pieces, (pgrad, *grads) = refs[:9], refs[9:19]
    ext, grad, win, stack, rows, field, update, amp, sems = refs[19:]
    n = points
    tiles = n // 128
    i = pl.program_id(0)

    @pl.when(i == 0)
    def _():
        copies = [
            pltpu.make_async_copy(piece, ext.at[:, pl.ds(r, h), pl.ds(c, w)], sems.at[k])
            for k, (piece, (r, h, c, w)) in enumerate(zip(pieces, spots))
        ]
        for copy in copies:
            copy.start()
        grad[...] = jnp.zeros(grad.shape, jnp.float32)
        pgrad[...] = jnp.zeros(pgrad.shape, jnp.float32)
        for copy in copies:
            copy.wait()

    def dot(x, y):
        return jnp.dot(x, y, preferred_element_type=jnp.float32)

    @pl.when(i < count[0])
    def _():
        slot = order[i]
        top = tops[slot]
        left = lefts[slot]
        base = pl.multiple_of(left // 128 * 128, 128)
        shift = left - base
        back = lax.rem(128 - shift, 128)
        floor = pl.multiple_of(top // 8 * 8, 8)
        low = top - floor
        up = lax.rem(8 - low, 8)
        lane = lax.broadcasted_iota(jnp.int32, (8, 128), 1)
        sub = lax.broadcasted_iota(jnp.int32, (8, 128), 0)
        keep = lane < 128 - shift
        upper = sub < 8 - low

        def strip(part, g):
            cols = [
                pltpu.roll(ext[part, pl.ds(floor + 8 * g, 8), pl.ds(base + 128 * j, 128)], back, 1)
                for j in range(tiles + 1)
            ]
            vals = [jnp.where(keep, cols[j], cols[j + 1]) for j in range(tiles)]
            return [pltpu.roll(v, up, 0) for v in vals]

        prev = [strip(part, 0) for part in range(2)]
        for k in range(n // 16):
            halves = []
            for h in range(2):
                following = [strip(part, 2 * k + h + 1) for part in range(2)]
                halves.append(
                    [
                        [jnp.where(upper, prev[part][j], following[part][j]) for j in range(tiles)]
                        for part in range(2)
                    ]
                )
                prev = following
            obj = [
                jnp.concatenate([jnp.concatenate(halves[h][part], 1) for h in range(2)], 0)
                for part in range(2)
            ]
            r = 16 * k
            for part in range(2):
                win[part, r : r + 16, :] = obj[part]
            for m in range(modes):
                p_re = probe[m, 0, r : r + 16, :]
                p_im = probe[m, 1, r : r + 16, :]
                psi_re = (p_re * obj[0] - p_im * obj[1]).astype(jnp.bfloat16)
                psi_im = (p_re * obj[1] + p_im * obj[0]).astype(jnp.bfloat16)
                stack[r : r + 16, m * n : (m + 1) * n] = psi_re
                stack[n + r : n + r + 16, m * n : (m + 1) * n] = psi_im
        first = dot(res[...], raw[0]).astype(jnp.bfloat16)
        second = dot(first, res_t[...])
        amp[...] = jnp.sqrt(jnp.maximum(second, 0.0)).astype(jnp.bfloat16).astype(jnp.float32)
        for m in range(modes):
            half_done = dot(fwd[...], stack[:, m * n : (m + 1) * n]).astype(jnp.bfloat16)
            rows[m * n : (m + 1) * n, 0:n] = half_done[:n]
            rows[m * n : (m + 1) * n, n : 2 * n] = half_done[n:]
        field[...] = dot(rows[...], bwd[...])
        for k in range(n // 8):
            r = 8 * k
            far = [field[m * n + r : m * n + r + 8, :] for m in range(modes)]
            total = far[0] * far[0]
            for m in range(1, modes):
                total = total + far[m] * far[m]
            total = total[:, :n] + total[:, n:]
            scaling = 1.0 - amp[r : r + 8, :] * lax.rsqrt(jnp.maximum(total, 1.0))
            scaling = jnp.concatenate([scaling, scaling], 1)
            for m in range(modes):
                rows[m * n + r : m * n + r + 8, :] = (far[m] * scaling).astype(jnp.bfloat16)
        for m in range(modes):
            turned = dot(rows[m * n : (m + 1) * n, :], fwd[...]).astype(jnp.bfloat16)
            stack[0:n, m * n : (m + 1) * n] = turned[:, :n]
            stack[n : 2 * n, m * n : (m + 1) * n] = turned[:, n:]
        update[...] = dot(bwd[...], stack[...])
        fresh = lane >= shift
        lower = sub >= low
        zero = jnp.zeros((8, 128), jnp.float32)
        last = [[zero] * tiles, [zero] * tiles]
        for g in range(n // 8 + 1):
            r = 8 * g
            if g < n // 8:
                o_re = win[0, r : r + 8, :]
                o_im = win[1, r : r + 8, :]
                t_re = t_im = None
                for m in range(modes):
                    u_re = update[r : r + 8, m * n : (m + 1) * n]
                    u_im = update[n + r : n + r + 8, m * n : (m + 1) * n]
                    p_re = probe[m, 0, r : r + 8, :]
                    p_im = probe[m, 1, r : r + 8, :]
                    a_re = p_re * u_re + p_im * u_im
                    a_im = p_re * u_im - p_im * u_re
                    t_re = a_re if t_re is None else t_re + a_re
                    t_im = a_im if t_im is None else t_im + a_im
                    pgrad[m, 0, r : r + 8, :] += o_re * u_re + o_im * u_im
                    pgrad[m, 1, r : r + 8, :] += o_re * u_im - o_im * u_re
                terms = [
                    [pltpu.roll(t[:, 128 * j : 128 * (j + 1)], low, 0) for j in range(tiles)]
                    for t in (t_re, t_im)
                ]
            else:
                terms = [[zero] * tiles, [zero] * tiles]
            for part in range(2):
                placed = [jnp.where(lower, terms[part][j], last[part][j]) for j in range(tiles)]
                turned = [zero] + [pltpu.roll(v, shift, 1) for v in placed] + [zero]
                for j in range(tiles + 1):
                    block = jnp.where(fresh, turned[j + 1], turned[j])
                    grad[part, pl.ds(floor + r, 8), pl.ds(base + 128 * j, 128)] += block
            last = terms

    @pl.when(i == pl.num_programs(0) - 1)
    def _():
        copies = [
            pltpu.make_async_copy(grad.at[:, pl.ds(r, h), pl.ds(c, w)], piece, sems.at[k])
            for k, (piece, (r, h, c, w)) in enumerate(zip(grads, spots))
        ]
        for copy in copies:
            copy.start()
        for copy in copies:
            copy.wait()


def run_frames(order, count, tops, lefts, raw, probe, fwd, bwd, res, res_t, pieces, half, tile):
    modes, _, n, _ = probe.shape
    spots = regions(half, tile)
    wide = tile + 2 * half
    anywhere = pl.BlockSpec(memory_space=pl.ANY)

    def whole(a):
        return pl.BlockSpec(a.shape, lambda i, *_: (0,) * a.ndim, pipeline_mode=pl.Buffered(1))

    outs = [jax.ShapeDtypeStruct(probe.shape, jnp.float32)]
    outs += [jax.ShapeDtypeStruct((2, h, w), jnp.float32) for _, h, _, w in spots]
    spec = pltpu.PrefetchScalarGridSpec(
        num_scalar_prefetch=4,
        grid=(raw.shape[0],),
        in_specs=[pl.BlockSpec((1, n, n), lambda i, order, *_: (order[i], 0, 0))]
        + [whole(a) for a in (probe, fwd, bwd, res, res_t)]
        + [anywhere] * 9,
        out_specs=[whole(outs[0])] + [anywhere] * 9,
        scratch_shapes=[
            pltpu.VMEM((2, wide, wide), jnp.float32),
            pltpu.VMEM((2, wide, wide), jnp.float32),
            pltpu.VMEM((2, n, n), jnp.float32),
            pltpu.VMEM((2 * n, modes * n), jnp.bfloat16),
            pltpu.VMEM((modes * n, 2 * n), jnp.bfloat16),
            pltpu.VMEM((modes * n, 2 * n), jnp.float32),
            pltpu.VMEM((2 * n, modes * n), jnp.float32),
            pltpu.VMEM((n, n), jnp.float32),
            pltpu.SemaphoreType.DMA((9,)),
        ],
    )
    return pl.pallas_call(
        functools.partial(frames_kernel, points=n, modes=modes, spots=spots),
        grid_spec=spec,
        out_shape=outs,
        compiler_params=pltpu.CompilerParams(
            dimension_semantics=("arbitrary",), vmem_limit_bytes=VMEM_BYTES
        ),
        name="frames",
    )(order, count, tops, lefts, raw, probe, fwd, bwd, res, res_t, *pieces)


def to_neighbour(value, step):
    rows, cols = lax.axis_size(ROW), lax.axis_size("col")
    pairs = [
        (r * cols + c, (r + step[0]) * cols + c + step[1])
        for r in range(rows)
        for c in range(cols)
        if 0 <= r + step[0] < rows and 0 <= c + step[1] < cols
    ]
    return lax.ppermute(value, ROW_COL, pairs)


def edge(value, step, width):
    for dim, s in ((1, step[0]), (2, step[1])):
        length = value.shape[dim]
        if s < 0:
            value = lax.slice_in_dim(value, 0, width, axis=dim)
        elif s > 0:
            value = lax.slice_in_dim(value, length - width, length, axis=dim)
    return value


def merge_kernel(own, *refs, half, tile):
    out = refs[-1]
    out[...] = own[...]
    span = {-1: (0, half), 0: (0, tile), 1: (tile - half, tile)}
    for piece, (a, b) in zip(refs[:-1], AROUND):
        (r0, r1), (c0, c1) = span[a], span[b]
        out[:, r0:r1, c0:c1] += piece[...]


def merge(own, pieces, half):
    def block(a):
        return pl.BlockSpec((1,) + a.shape[1:], lambda i: (i, 0, 0))

    return pl.pallas_call(
        functools.partial(merge_kernel, half=half, tile=own.shape[1]),
        grid=(own.shape[0],),
        in_specs=[block(own)] + [block(p) for p in pieces],
        out_specs=block(own),
        out_shape=jax.ShapeDtypeStruct(own.shape, own.dtype),
        compiler_params=pltpu.CompilerParams(
            dimension_semantics=("arbitrary",), vmem_limit_bytes=VMEM_BYTES
        ),
        name="merge",
    )(own, *pieces)


def sum_over_devices(value, halved, whole, scale):
    taken = []
    for axis, bit in halved:
        size = lax.axis_size(axis)
        side = lax.axis_index(axis) // bit % 2
        pairs = [(j, j ^ bit) for j in range(size)]
        length = value.shape[0] // 2
        mine = lax.dynamic_slice_in_dim(value, side * length, length, 0)
        other = lax.dynamic_slice_in_dim(value, (1 - side) * length, length, 0)
        value = mine + lax.ppermute(other, axis, pairs)
        taken.append((axis, pairs, side))
    for axis, bit in whole:
        pairs = [(j, j ^ bit) for j in range(lax.axis_size(axis))]
        value = value + lax.ppermute(value, axis, pairs)
    value = value * scale
    for axis, pairs, side in reversed(taken):
        other = lax.ppermute(value, axis, pairs)
        value = jnp.where(
            side == 0, jnp.concatenate([value, other], 0), jnp.concatenate([other, value], 0)
        )
    return value


def shards(object_field, probe, raw_counts, resample_delta, tile_row, offsets):
    modes, _, points, _ = probe.shape
    half = points // 2
    tile = object_field.shape[1]
    tile_rows = lax.axis_size(ROW)
    frame_total = raw_counts.shape[0] * tile_rows * lax.axis_size("col")
    target = tile_row[:, 0]
    slots = spread(target, raw_counts, tile_rows)
    slot_ids = jnp.arange(tile_rows, dtype=jnp.int32)
    picks = (target[:, None] == slot_ids[None, :]).astype(jnp.int32)
    requests = jnp.stack(
        [jnp.sum(picks * offsets[:, 0:1], 0), jnp.sum(picks * offsets[:, 1:2], 0), jnp.sum(picks, 0)], 1
    )
    received = lax.all_to_all(requests, ROW, split_axis=0, concat_axis=0, tiled=True)
    arrived = lax.all_to_all(slots, ROW, split_axis=0, concat_axis=0, tiled=True)
    around = [to_neighbour(edge(object_field, (-a, -b), half), (-a, -b)) for a, b in AROUND]
    live = received[:, 2]
    count = jnp.sum(live)
    rank = jnp.sum(jnp.where(slot_ids[None, :] < slot_ids[:, None], live[None, :], 0), 1)
    place = jnp.minimum(slot_ids, jnp.maximum(count - 1, 0))
    hit = (rank[None, :] == place[:, None]) & (live[None, :] > 0)
    order = jnp.sum(jnp.where(hit, slot_ids[None, :], 0), 1)
    forward, backward = dft_tables(points)
    resample = (jnp.eye(points, dtype=jnp.float32) + resample_delta).astype(jnp.bfloat16)
    probe_total, own, *outer = run_frames(
        order, count[None], received[:, 0], received[:, 1], arrived, probe, forward, backward,
        resample, resample.T, [object_field] + around, half, tile,
    )
    halved = (("row_2", 1), ("col", 1), ("col", 2))
    whole = (("col", 4), ("row_1", 1), ("row_0", 1), ("row_0", 2))
    probe_grad = sum_over_devices(
        probe_total.reshape(-1, points), halved, whole, 1.0 / math.sqrt(frame_total)
    ).reshape(probe.shape)
    inward = [to_neighbour(piece, step) for piece, step in zip(outer, AROUND)]
    back = [inward[AROUND.index((-a, -b))] for a, b in AROUND]
    object_grad = merge(own, back, half)
    return (object_grad, probe_grad)


def solution(mesh):
    torus = Mesh(
        mesh.devices.reshape(4, 2, 2, mesh.shape["col"]), ("row_0", "row_1", "row_2", "col")
    )
    return jax.shard_map(
        shards,
        mesh=torus,
        in_specs=(
            P(None, ROW, "col"),
            P(),
            P(ROW_COL, None, None),
            P(),
            P(ROW_COL, None),
            P(ROW_COL, None),
        ),
        out_specs=(P(None, ROW, "col"), P()),
        check_vma=False,
    )
```

time: 1080 us -> 299 us (0.28); the launches traced: 1070 us -> 298 us
  waiting for transfers between devices: 434 us -> 102 us
  local copies, waits for them, and re-layouts: 317 us -> 8.7 us
  other arithmetic: 154 us -> 8.38 us
  starting transfers between devices: 50.1 us -> 119 us
  Pallas kernels: 0 us -> 58.1 us
  loops' own time: 54.8 us -> 0 us
  matrix products: 40.6 us -> 0 us
  between operations: 14.4 us -> 1.91 us
    all_to_all x3 -> x2, waiting for transfers between devices: 261 us -> 0.01 us  [the longest x1 0.01 us: shards(): lax.all_to_all(requests, ROW, split_axis=0, concat_axis=0, tiled=True)]
    psum x1 -> x0, waiting for transfers between devices: 140 us -> none  [shards(): probe_grad = lax.psum(probe_total, ROW_COL) * (1.0 / math.sqrt(frame_total))]
    dynamic_update_slice x28 -> x0, local copies, waits for them, and re-layouts: 122 us -> none  [the longest x16 98.6 us: place(): lax.dynamic_update_slice(gradient, current + term, (anchor, top, left))]
    ppermute x8 -> x26, starting transfers between devices: 17.7 us -> 105 us  [the longest x16 48.8 us: to_neighbour(): return lax.ppermute(value, ROW_COL, pairs)]
    gather x49 -> x0, local copies, waits for them, and re-layouts: 70.8 us -> none
    ppermute x8 -> x26, waiting for transfers between devices: 32.5 us -> 102 us  [the longest x16 60.7 us: to_neighbour(): return lax.ppermute(value, ROW_COL, pairs)]
    pallas_call x0 -> x3, Pallas kernels: none -> 58.1 us  [the longest x1 29.1 us: run_frames(): pl.pallas_call(functools.partial(frames_kernel, points=n, modes=modes, sp...]
    another operation x3 -> x0, loops' own time: 54.8 us -> none  [the longest x1 53.7 us: shards(): gradient = lax.fori_loop(0, tile_rows, add_slot, zero_grad)]
  transfers between devices with their start and end apart: 12 -> 28, of which waited for: 7 -> 15; matrix products, arithmetic and copies ran while one was open for 2% -> 3% of each run, Pallas kernels for 0% -> 10%
where the time goes in v1:
time: 299 us; the launch traced here: 298 us
  starting transfers between devices  119 us (40%)
  waiting for transfers between devices  102 us (34%)
  Pallas kernels  58.1 us (19%)
  local copies, waits for them, and re-layouts  8.7 us (3%)
  other arithmetic  8.38 us (3%)
    ppermute x16, waiting for transfers between devices, to_neighbour(): return lax.ppermute(value, ROW_COL, pairs)  60.7 us
    ppermute x16, starting transfers between devices, to_neighbour(): return lax.ppermute(value, ROW_COL, pairs)  48.8 us
    ppermute x4, starting transfers between devices, sum_over_devices(): value = value + lax.ppermute(value, axis, pairs)  34.1 us
    pallas_call x1, Pallas kernels, run_frames(): pl.pallas_call(functools.partial(frames_kernel, points=n, modes=modes, sp...  29.1 us
    pallas_call x1, Pallas kernels, spread(): pl.pallas_call(spread_kernel, grid_spec=pltpu.PrefetchScalarGridSpec(num_...  25.6 us
    ppermute x3, waiting for transfers between devices, sum_over_devices(): value = mine + lax.ppermute(other, axis, pairs)  17.4 us
    ppermute x4, waiting for transfers between devices, sum_over_devices(): value = value + lax.ppermute(value, axis, pairs)  14 us
    ppermute x3, starting transfers between devices, sum_over_devices(): value = mine + lax.ppermute(other, axis, pairs)  12.6 us
  transfers between devices with their start and end apart: 28, of which 15 were waited for; matrix products, arithmetic and copies ran while one was open for 3% of the time, Pallas kernels for 10%

profile of v1, /device:TPU:1, one launch (start us, length us, event | category | flops | bytes accessed | tf_op | source)
XLA Modules:
  0.0 298.4 jit_solution(555522771235524009)
XLA Ops:
  2.8 8.4 %all-to-all-start = ((s32[16,1,3]{2,1,0:T(1,128)}), s32[16,1,3]{2,1,0:T(1,128)S(1)}, u32[]{:S(2)}, u32[]{:S(2)}) async-start(s32[16,1,3]{2,1,0:T(1,128)} %copy.14), calls=%async_computation | async-start | bytes 16384 | tf_op jit(solution)/shard_map/all_to_all | solution.py:332
  13.2 4.9 %collective-permute-start = (f32[2,128,128]{2,1,0:T(8,128)}, f32[2,128,128]{2,1,0:T(8,128)S(1)}, u32[]{:S(2)}, u32[]{:S(2)}) collective-permute-start(f32[2,128,128]{2,1,0:T(8,128)} %get-tuple-element.28), channel_id=1, source_target_pairs={{0,9},{1,10},{2,11},{3,12},{4,13},{5,14},{6,15},{8,17},{9,18},{10,... | collective-permute-start | bytes 393224 | tf_op jit(solution)/shard_map/ppermute | solution.py:257
  18.1 25.6 %spread.1 = bf16[16,256,256]{2,1,0:T(8,128)(2,1)} custom-call(s32[6]{0:T(128)} %bitcast.30, bf16[6,256,256]{2,1,0:T(8,128)(2,1)} %counts.1), custom_call_target="tpu_custom_call" | custom-call | tf_op jit(solution)/shard_map/spread/pallas_call | solution.py:45
  43.8 5.5 %all-to-all-start.1 = ((bf16[16,256,256]{2,1,0:T(8,128)(2,1)}), bf16[16,256,256]{2,1,0:T(8,128)(2,1)}, u32[]{:S(2)}, u32[]{:S(2)}) async-start(bf16[16,256,256]{2,1,0:T(8,128)(2,1)} %spread.1), calls=%async_computation.1 | async-start | bytes 4194304 | tf_op jit(solution)/shard_map/all_to_all | solution.py:333
  49.3 5.2 %collective-permute-start.1 = (f32[2,128,512]{2,1,0:T(8,128)S(1)}, f32[2,128,512]{2,1,0:T(8,128)}, u32[]{:S(2)}, u32[]{:S(2)}) collective-permute-start(f32[2,128,512]{2,1,0:T(8,128)S(1)} %get-tuple-element.30), channel_id=1, source_target_pairs={{0,8},{1,9},{2,10},{3,11},{4,12},{5,13},{6,14},{7,15},{8,16},{9,17... | collective-permute-start | bytes 1572872 | tf_op jit(solution)/shard_map/ppermute | solution.py:257
  56.9 4.0 %collective-permute-start.3 = (f32[2,512,128]{2,1,0:T(8,128)}, f32[2,512,128]{2,1,0:T(8,128)S(1)}, u32[]{:S(2)}, u32[]{:S(2)}) collective-permute-start(f32[2,512,128]{2,1,0:T(8,128)} %get-tuple-element.32), channel_id=1, source_target_pairs={{0,1},{1,2},{2,3},{3,4},{4,5},{5,6},{6,7},{8,9},{9,10},{10,11},{11... | collective-permute-start | bytes 1572872 | tf_op jit(solution)/shard_map/ppermute | solution.py:257
  68.5 6.1 %collective-permute-start.5 = (f32[2,128,128]{2,1,0:T(8,128)S(1)}, f32[2,128,128]{2,1,0:T(8,128)S(1)}, u32[]{:S(2)}, u32[]{:S(2)}) collective-permute-start(f32[2,128,128]{2,1,0:T(8,128)S(1)} %copy-done.13), channel_id=1, source_target_pairs={{8,1},{9,2},{10,3},{11,4},{12,5},{13,6},{14,7},{16,9},{17,10},{18,... | collective-permute-start | bytes 393224 | tf_op jit(solution)/shard_map/ppermute | solution.py:257
  77.3 20.3 %collective-permute-done.5.refs_6_ = f32[2,128,128]{2,1,0:T(8,128)S(1)} collective-permute-done((f32[2,128,128]{2,1,0:T(8,128)S(1)}, f32[2,128,128]{2,1,0:T(8,128)S(1)}, u32[]{:S(2)}, u32[]{:S(2)}) %collective-permute-start.5) | collective-permute-done | bytes 131104 | tf_op jit(solution)/shard_map/ppermute | solution.py:257
  99.5 5.5 %collective-permute-done.7.refs_8_ = f32[2,128,128]{2,1,0:T(8,128)S(1)} collective-permute-done((f32[2,128,128]{2,1,0:T(8,128)S(1)}, f32[2,128,128]{2,1,0:T(8,128)S(1)}, u32[]{:S(2)}, u32[]{:S(2)}) %collective-permute-start.7) | collective-permute-done | bytes 131104 | tf_op jit(solution)/shard_map/ppermute | solution.py:257
  105.1 5.3 %collective-permute-done.4.refs_5_ = f32[2,512,128]{2,1,0:T(8,128)S(1)} collective-permute-done((f32[2,512,128]{2,1,0:T(8,128)}, f32[2,512,128]{2,1,0:T(8,128)S(1)}, u32[]{:S(2)}, u32[]{:S(2)}) %collective-permute-start.4) | collective-permute-done | bytes 524320 | tf_op jit(solution)/shard_map/ppermute | solution.py:257
  111.4 29.1 %frames.1 = (f32[3,2,256,256]{3,2,1,0:T(8,128)}, f32[2,512,512]{2,1,0:T(8,128)}, f32[2,128,128]{2,1,0:T(8,128)}, f32[2,128,512]{2,1,0:T(8,128)}, f32[2,128,128]{...) custom-call(s32[16]{0:T(128)} %select_reduce_fusion.order, ...), custom_call_target="tpu_custom_call" | custom-call | tf_op jit(solution)/shard_map/frames/pallas_call | solution.py:238
  141.8 12.4 %collective-permute-start.16 = (f32[768,256]{1,0:T(8,128)S(1)}, f32[768,256]{1,0:T(8,128)S(1)}, u32[]{:S(2)}, u32[]{:S(2)}) collective-permute-start(f32[768,256]{1,0:T(8,128)S(1)} %constant_dynamic-slice_fusion.2), channel_id=1, source_target_pairs={{0,8},{8,0},{1,9},{9,1},{2,10},{10,2},{3,11},{11,3},{4,12},{12,4},... | collective-permute-start | bytes 2359304 | tf_op jit(solution)/shard_map/ppermute | solution.py:305
  156.4 10.3 %collective-permute-done.17 = f32[384,256]{1,0:T(8,128)S(1)} collective-permute-done((f32[384,256]{1,0:T(8,128)S(1)}, f32[384,256]{1,0:T(8,128)S(1)}, u32[]{:S(2)}, u32[]{:S(2)}) %collective-permute-start.17) | collective-permute-done | bytes 393248 | tf_op jit(solution)/shard_map/ppermute | solution.py:305
  166.9 5.2 %collective-permute-done.18 = f32[192,256]{1,0:T(8,128)S(1)} collective-permute-done((f32[192,256]{1,0:T(8,128)S(1)}, f32[192,256]{1,0:T(8,128)S(1)}, u32[]{:S(2)}, u32[]{:S(2)}) %collective-permute-start.18) | collective-permute-done | bytes 196640 | tf_op jit(solution)/shard_map/ppermute | solution.py:305
  174.1 4.1 %collective-permute-done.19 = f32[192,256]{1,0:T(8,128)S(1)} collective-permute-done((f32[192,256]{1,0:T(8,128)S(1)}, f32[192,256]{1,0:T(8,128)S(1)}, u32[]{:S(2)}, u32[]{:S(2)}) %collective-permute-start.19) | collective-permute-done | bytes 196640 | tf_op jit(solution)/shard_map/ppermute | solution.py:309
  178.2 10.7 %collective-permute-start.20 = (f32[192,256]{1,0:T(8,128)S(1)}, f32[192,256]{1,0:T(8,128)S(1)}, u32[]{:S(2)}, u32[]{:S(2)}) collective-permute-start(f32[192,256]{1,0:T(8,128)S(1)} %add.90), channel_id=1, source_target_pairs={{0,16},{16,0},{1,17},{17,1},{2,18},{18,2},{3,19},{19,3},{4,20},{20... | collective-permute-start | bytes 589832 | tf_op jit(solution)/shard_map/ppermute | solution.py:309
  196.9 19.6 %collective-permute-start.22 = (f32[192,256]{1,0:T(8,128)S(1)}, f32[192,256]{1,0:T(8,128)S(1)}, u32[]{:S(2)}, u32[]{:S(2)}) collective-permute-start(f32[192,256]{1,0:T(8,128)S(1)} %add.92), channel_id=1, source_target_pairs={{0,64},{32,96},{64,0},{96,32},{1,65},{33,97},{65,1},{97,33},{2,66}... | collective-permute-start | bytes 589832 | tf_op jit(solution)/shard_map/ppermute | solution.py:309
  225.6 6.3 %collective-permute-done.24 = f32[384,256]{1,0:T(8,128)S(1)} collective-permute-done((f32[384,256]{1,0:T(8,128)S(1)}, f32[384,256]{1,0:T(8,128)S(1)}, u32[]{:S(2)}, u32[]{:S(2)}) %collective-permute-start.24) | collective-permute-done | bytes 393248 | tf_op jit(solution)/shard_map/ppermute | solution.py:312
  232.0 8.3 %collective-permute-start.25 = (f32[768,256]{1,0:T(8,128)S(1)}, f32[768,256]{1,0:T(8,128)S(1)}, u32[]{:S(2)}, u32[]{:S(2)}) collective-permute-start(f32[768,256]{1,0:T(8,128)S(1)} %maximum_select_fusion.1), channel_id=1, source_target_pairs={{0,8},{8,0},{1,9},{9,1},{2,10},{10,2},{3,11},{11,3},{4,12},{12,4},... | collective-permute-start | bytes 2359304 | tf_op jit(solution)/shard_map/ppermute | solution.py:312
  240.3 4.3 %collective-permute-start.8 = (f32[2,128,128]{2,1,0:T(8,128)S(1)}, f32[2,128,128]{2,1,0:T(8,128)S(1)}, u32[]{:S(2)}, u32[]{:S(2)}) collective-permute-start(f32[2,128,128]{2,1,0:T(8,128)S(1)} %copy-done.19), channel_id=1, source_target_pairs={{0,9},{1,10},{2,11},{3,12},{4,13},{5,14},{6,15},{8,17},{9,18},{10,... | collective-permute-start | bytes 393224 | tf_op jit(solution)/shard_map/ppermute | solution.py:257
  245.9 4.3 %collective-permute-start.13 = (f32[2,128,128]{2,1,0:T(8,128)S(1)}, f32[2,128,128]{2,1,0:T(8,128)S(1)}, u32[]{:S(2)}, u32[]{:S(2)}) collective-permute-start(f32[2,128,128]{2,1,0:T(8,128)S(1)} %copy-done.17), channel_id=1, source_target_pairs={{8,1},{9,2},{10,3},{11,4},{12,5},{13,6},{14,7},{16,9},{17,10},{18,... | collective-permute-start | bytes 393224 | tf_op jit(solution)/shard_map/ppermute | solution.py:257
  254.9 5.1 %collective-permute-start.11 = (f32[2,512,128]{2,1,0:T(8,128)}, f32[2,512,128]{2,1,0:T(8,128)S(1)}, u32[]{:S(2)}, u32[]{:S(2)}) collective-permute-start(f32[2,512,128]{2,1,0:T(8,128)} %get-tuple-element.16), channel_id=1, source_target_pairs={{0,1},{1,2},{2,3},{3,4},{4,5},{5,6},{6,7},{8,9},{9,10},{10,11},{11... | collective-permute-start | bytes 1572872 | tf_op jit(solution)/shard_map/ppermute | solution.py:257
  263.5 14.7 %collective-permute-done.11.refs_3_ = f32[2,512,128]{2,1,0:T(8,128)S(1)} collective-permute-done((f32[2,512,128]{2,1,0:T(8,128)}, f32[2,512,128]{2,1,0:T(8,128)S(1)}, u32[]{:S(2)}, u32[]{:S(2)}) %collective-permute-start.11) | collective-permute-done | bytes 524320 | tf_op jit(solution)/shard_map/ppermute | solution.py:257
  278.2 14.7 %collective-permute-done.12.refs_4_ = f32[2,512,128]{2,1,0:T(8,128)S(1)} collective-permute-done((f32[2,512,128]{2,1,0:T(8,128)}, f32[2,512,128]{2,1,0:T(8,128)S(1)}, u32[]{:S(2)}, u32[]{:S(2)}) %collective-permute-start.12) | collective-permute-done | bytes 524320 | tf_op jit(solution)/shard_map/ppermute | solution.py:257
  (108 shorter events, 56.9 us)
Async XLA Ops:
  2.8 40.9 %all-to-all-start = ((s32[16,1,3]{2,1,0:T(1,128)}), s32[16,1,3]{2,1,0:T(1,128)S(1)}, u32[]{:S(2)}, u32[]{:S(2)}) async-start(s32[16,1,3]{2,1,0:T(1,128)} %copy.14), calls=%async_computation | async-start | bytes 16384 | tf_op jit(solution)/shard_map/all_to_all | solution.py:332
  13.2 55.2 %collective-permute-start = (f32[2,128,128]{2,1,0:T(8,128)}, f32[2,128,128]{2,1,0:T(8,128)S(1)}, u32[]{:S(2)}, u32[]{:S(2)}) collective-permute-start(f32[2,128,128]{2,1,0:T(8,128)} %get-tuple-element.28), channel_id=1, source_target_pairs={{0,9},{1,10},{2,11},{3,12},{4,13},{5,14},{6,15},{8,17},{9,18},{10,... | collective-permute-start | bytes 393224 | tf_op jit(solution)/shard_map/ppermute | solution.py:257
  43.8 66.5 %all-to-all-start.1 = ((bf16[16,256,256]{2,1,0:T(8,128)(2,1)}), bf16[16,256,256]{2,1,0:T(8,128)(2,1)}, u32[]{:S(2)}, u32[]{:S(2)}) async-start(bf16[16,256,256]{2,1,0:T(8,128)(2,1)} %spread.1), calls=%async_computation.1 | async-start | bytes 4194304 | tf_op jit(solution)/shard_map/all_to_all | solution.py:333
  49.3 55.7 %collective-permute-start.1 = (f32[2,128,512]{2,1,0:T(8,128)S(1)}, f32[2,128,512]{2,1,0:T(8,128)}, u32[]{:S(2)}, u32[]{:S(2)}) collective-permute-start(f32[2,128,512]{2,1,0:T(8,128)S(1)} %get-tuple-element.30), channel_id=1, source_target_pairs={{0,8},{1,9},{2,10},{3,11},{4,12},{5,13},{6,14},{7,15},{8,16},{9,17... | collective-permute-start | bytes 1572872 | tf_op jit(solution)/shard_map/ppermute | solution.py:257
  54.5 20.0 %collective-permute-start.2 = (f32[2,128,128]{2,1,0:T(8,128)}, f32[2,128,128]{2,1,0:T(8,128)}, u32[]{:S(2)}, u32[]{:S(2)}) collective-permute-start(f32[2,128,128]{2,1,0:T(8,128)} %get-tuple-element.27), channel_id=1, source_target_pairs={{1,8},{2,9},{3,10},{4,11},{5,12},{6,13},{7,14},{9,16},{10,17},{11,... | collective-permute-start | bytes 393224 | tf_op jit(solution)/shard_map/ppermute | solution.py:257
  56.9 48.2 %collective-permute-start.3 = (f32[2,512,128]{2,1,0:T(8,128)}, f32[2,512,128]{2,1,0:T(8,128)S(1)}, u32[]{:S(2)}, u32[]{:S(2)}) collective-permute-start(f32[2,512,128]{2,1,0:T(8,128)} %get-tuple-element.32), channel_id=1, source_target_pairs={{0,1},{1,2},{2,3},{3,4},{4,5},{5,6},{6,7},{8,9},{9,10},{10,11},{11... | collective-permute-start | bytes 1572872 | tf_op jit(solution)/shard_map/ppermute | solution.py:257
  60.9 49.4 %collective-permute-start.4 = (f32[2,512,128]{2,1,0:T(8,128)}, f32[2,512,128]{2,1,0:T(8,128)S(1)}, u32[]{:S(2)}, u32[]{:S(2)}) collective-permute-start(f32[2,512,128]{2,1,0:T(8,128)} %get-tuple-element.31), channel_id=1, source_target_pairs={{1,0},{2,1},{3,2},{4,3},{5,4},{6,5},{7,6},{9,8},{10,9},{11,10},{12... | collective-permute-start | bytes 1572872 | tf_op jit(solution)/shard_map/ppermute | solution.py:257
  68.5 29.1 %collective-permute-start.5 = (f32[2,128,128]{2,1,0:T(8,128)S(1)}, f32[2,128,128]{2,1,0:T(8,128)S(1)}, u32[]{:S(2)}, u32[]{:S(2)}) collective-permute-start(f32[2,128,128]{2,1,0:T(8,128)S(1)} %copy-done.13), channel_id=1, source_target_pairs={{8,1},{9,2},{10,3},{11,4},{12,5},{13,6},{14,7},{16,9},{17,10},{18,... | collective-permute-start | bytes 393224 | tf_op jit(solution)/shard_map/ppermute | solution.py:257
  74.5 35.8 %collective-permute-start.6 = (f32[2,128,512]{2,1,0:T(8,128)S(1)}, f32[2,128,512]{2,1,0:T(8,128)S(1)}, u32[]{:S(2)}, u32[]{:S(2)}) collective-permute-start(f32[2,128,512]{2,1,0:T(8,128)S(1)} %get-tuple-element.29), channel_id=1, source_target_pairs={{8,0},{9,1},{10,2},{11,3},{12,4},{13,5},{14,6},{15,7},{16,8},{17,9... | collective-permute-start | bytes 1572872 | tf_op jit(solution)/shard_map/ppermute | solution.py:257
  97.6 7.5 %collective-permute-start.7 = (f32[2,128,128]{2,1,0:T(8,128)S(1)}, f32[2,128,128]{2,1,0:T(8,128)S(1)}, u32[]{:S(2)}, u32[]{:S(2)}) collective-permute-start(f32[2,128,128]{2,1,0:T(8,128)S(1)} %copy-done.12), channel_id=1, source_target_pairs={{9,0},{10,1},{11,2},{12,3},{13,4},{14,5},{15,6},{17,8},{18,9},{19,... | collective-permute-start | bytes 393224 | tf_op jit(solution)/shard_map/ppermute | solution.py:257
  141.8 14.3 %collective-permute-start.16 = (f32[768,256]{1,0:T(8,128)S(1)}, f32[768,256]{1,0:T(8,128)S(1)}, u32[]{:S(2)}, u32[]{:S(2)}) collective-permute-start(f32[768,256]{1,0:T(8,128)S(1)} %constant_dynamic-slice_fusion.2), channel_id=1, source_target_pairs={{0,8},{8,0},{1,9},{9,1},{2,10},{10,2},{3,11},{11,3},{4,12},{12,4},... | collective-permute-start | bytes 2359304 | tf_op jit(solution)/shard_map/ppermute | solution.py:305
  156.3 10.4 %collective-permute-start.17 = (f32[384,256]{1,0:T(8,128)S(1)}, f32[384,256]{1,0:T(8,128)S(1)}, u32[]{:S(2)}, u32[]{:S(2)}) collective-permute-start(f32[384,256]{1,0:T(8,128)S(1)} %constant_dynamic-slice_fusion.1), channel_id=1, source_target_pairs={{0,1},{1,0},{2,3},{3,2},{4,5},{5,4},{6,7},{7,6},{8,9},{9,8},{10,11... | collective-permute-start | bytes 1179656 | tf_op jit(solution)/shard_map/ppermute | solution.py:305
  178.2 13.7 %collective-permute-start.20 = (f32[192,256]{1,0:T(8,128)S(1)}, f32[192,256]{1,0:T(8,128)S(1)}, u32[]{:S(2)}, u32[]{:S(2)}) collective-permute-start(f32[192,256]{1,0:T(8,128)S(1)} %add.90), channel_id=1, source_target_pairs={{0,16},{16,0},{1,17},{17,1},{2,18},{18,2},{3,19},{19,3},{4,20},{20... | collective-permute-start | bytes 589832 | tf_op jit(solution)/shard_map/ppermute | solution.py:309
  196.9 23.4 %collective-permute-start.22 = (f32[192,256]{1,0:T(8,128)S(1)}, f32[192,256]{1,0:T(8,128)S(1)}, u32[]{:S(2)}, u32[]{:S(2)}) collective-permute-start(f32[192,256]{1,0:T(8,128)S(1)} %add.92), channel_id=1, source_target_pairs={{0,64},{32,96},{64,0},{96,32},{1,65},{33,97},{65,1},{97,33},{2,66}... | collective-permute-start | bytes 589832 | tf_op jit(solution)/shard_map/ppermute | solution.py:309
  225.2 6.7 %collective-permute-start.24 = (f32[384,256]{1,0:T(8,128)S(1)}, f32[384,256]{1,0:T(8,128)S(1)}, u32[]{:S(2)}, u32[]{:S(2)}) collective-permute-start(f32[384,256]{1,0:T(8,128)S(1)} %maximum_select_fusion.2), channel_id=1, source_target_pairs={{0,1},{1,0},{2,3},{3,2},{4,5},{5,4},{6,7},{7,6},{8,9},{9,8},{10,11... | collective-permute-start | bytes 1179656 | tf_op jit(solution)/shard_map/ppermute | solution.py:312
  232.0 65.2 %collective-permute-start.25 = (f32[768,256]{1,0:T(8,128)S(1)}, f32[768,256]{1,0:T(8,128)S(1)}, u32[]{:S(2)}, u32[]{:S(2)}) collective-permute-start(f32[768,256]{1,0:T(8,128)S(1)} %maximum_select_fusion.1), channel_id=1, source_target_pairs={{0,8},{8,0},{1,9},{9,1},{2,10},{10,2},{3,11},{11,3},{4,12},{12,4},... | collective-permute-start | bytes 2359304 | tf_op jit(solution)/shard_map/ppermute | solution.py:312
  240.3 11.2 %collective-permute-start.8 = (f32[2,128,128]{2,1,0:T(8,128)S(1)}, f32[2,128,128]{2,1,0:T(8,128)S(1)}, u32[]{:S(2)}, u32[]{:S(2)}) collective-permute-start(f32[2,128,128]{2,1,0:T(8,128)S(1)} %copy-done.19), channel_id=1, source_target_pairs={{0,9},{1,10},{2,11},{3,12},{4,13},{5,14},{6,15},{8,17},{9,18},{10,... | collective-permute-start | bytes 393224 | tf_op jit(solution)/shard_map/ppermute | solution.py:257
  244.5 10.4 %collective-permute-start.10 = (f32[2,128,128]{2,1,0:T(8,128)S(1)}, f32[2,128,128]{2,1,0:T(8,128)S(1)}, u32[]{:S(2)}, u32[]{:S(2)}) collective-permute-start(f32[2,128,128]{2,1,0:T(8,128)S(1)} %copy-done.18), channel_id=1, source_target_pairs={{1,8},{2,9},{3,10},{4,11},{5,12},{6,13},{7,14},{9,16},{10,17},{11,... | collective-permute-start | bytes 393224 | tf_op jit(solution)/shard_map/ppermute | solution.py:257
  245.9 14.2 %collective-permute-start.13 = (f32[2,128,128]{2,1,0:T(8,128)S(1)}, f32[2,128,128]{2,1,0:T(8,128)S(1)}, u32[]{:S(2)}, u32[]{:S(2)}) collective-permute-start(f32[2,128,128]{2,1,0:T(8,128)S(1)} %copy-done.17), channel_id=1, source_target_pairs={{8,1},{9,2},{10,3},{11,4},{12,5},{13,6},{14,7},{16,9},{17,10},{18,... | collective-permute-start | bytes 393224 | tf_op jit(solution)/shard_map/ppermute | solution.py:257
  250.1 11.2 %collective-permute-start.15 = (f32[2,128,128]{2,1,0:T(8,128)}, f32[2,128,128]{2,1,0:T(8,128)}, u32[]{:S(2)}, u32[]{:S(2)}) collective-permute-start(f32[2,128,128]{2,1,0:T(8,128)} %get-tuple-element.20), channel_id=1, source_target_pairs={{9,0},{10,1},{11,2},{12,3},{13,4},{14,5},{15,6},{17,8},{18,9},{19,... | collective-permute-start | bytes 393224 | tf_op jit(solution)/shard_map/ppermute | solution.py:257
  251.5 12.1 %collective-permute-start.9 = (f32[2,128,512]{2,1,0:T(8,128)}, f32[2,128,512]{2,1,0:T(8,128)S(1)}, u32[]{:S(2)}, u32[]{:S(2)}) collective-permute-start(f32[2,128,512]{2,1,0:T(8,128)} %get-tuple-element.14), channel_id=1, source_target_pairs={{0,8},{1,9},{2,10},{3,11},{4,12},{5,13},{6,14},{7,15},{8,16},{9,17... | collective-permute-start | bytes 1572872 | tf_op jit(solution)/shard_map/ppermute | solution.py:257
  254.9 23.3 %collective-permute-start.11 = (f32[2,512,128]{2,1,0:T(8,128)}, f32[2,512,128]{2,1,0:T(8,128)S(1)}, u32[]{:S(2)}, u32[]{:S(2)}) collective-permute-start(f32[2,512,128]{2,1,0:T(8,128)} %get-tuple-element.16), channel_id=1, source_target_pairs={{0,1},{1,2},{2,3},{3,4},{4,5},{5,6},{6,7},{8,9},{9,10},{10,11},{11... | collective-permute-start | bytes 1572872 | tf_op jit(solution)/shard_map/ppermute | solution.py:257
  260.1 32.9 %collective-permute-start.12 = (f32[2,512,128]{2,1,0:T(8,128)}, f32[2,512,128]{2,1,0:T(8,128)S(1)}, u32[]{:S(2)}, u32[]{:S(2)}) collective-permute-start(f32[2,512,128]{2,1,0:T(8,128)} %get-tuple-element.17), channel_id=1, source_target_pairs={{1,0},{2,1},{3,2},{4,3},{5,4},{6,5},{7,6},{9,8},{10,9},{11,10},{12... | collective-permute-start | bytes 1572872 | tf_op jit(solution)/shard_map/ppermute | solution.py:257
  261.4 31.6 %collective-permute-start.14 = (f32[2,128,512]{2,1,0:T(8,128)}, f32[2,128,512]{2,1,0:T(8,128)}, u32[]{:S(2)}, u32[]{:S(2)}) collective-permute-start(f32[2,128,512]{2,1,0:T(8,128)} %get-tuple-element.19), channel_id=1, source_target_pairs={{8,0},{9,1},{10,2},{11,3},{12,4},{13,5},{14,6},{15,7},{16,8},{17,9... | collective-permute-start | bytes 1572872 | tf_op jit(solution)/shard_map/ppermute | solution.py:257
  (24 other events, 461.1 us)

commit v2 on v1

--- a/solution.py
+++ b/solution.py
@@ -31,25 +31,19 @@
     return (forward.astype(jnp.bfloat16), backward.astype(jnp.bfloat16))
 
 
-def spread_kernel(target, counts, slots, sems):
-    copies = [
-        pltpu.make_async_copy(counts.at[j], slots.at[target[j]], sems.at[j]) for j in range(counts.shape[0])
-    ]
-    for copy in copies:
-        copy.start()
-    for copy in copies:
-        copy.wait()
+def spread_kernel(target, frame, slot):
+    slot[...] = frame[...]
 
 
 def spread(target, counts, slot_count):
+    block = (1,) + counts.shape[1:]
     return pl.pallas_call(
         spread_kernel,
         grid_spec=pltpu.PrefetchScalarGridSpec(
             num_scalar_prefetch=1,
-            grid=(1,),
-            in_specs=[pl.BlockSpec(memory_space=pl.ANY)],
-            out_specs=pl.BlockSpec(memory_space=pl.ANY),
-            scratch_shapes=[pltpu.SemaphoreType.DMA((counts.shape[0],))],
+            grid=(counts.shape[0],),
+            in_specs=[pl.BlockSpec(block, lambda j, target: (j, 0, 0))],
+            out_specs=pl.BlockSpec(block, lambda j, target: (target[j], 0, 0)),
         ),
         out_shape=jax.ShapeDtypeStruct((slot_count,) + counts.shape[1:], counts.dtype),
         name="spread",
@@ -293,27 +287,41 @@
     )(own, *pieces)
 
 
-def sum_over_devices(value, halved, whole, scale):
-    taken = []
-    for axis, bit in halved:
-        size = lax.axis_size(axis)
-        side = lax.axis_index(axis) // bit % 2
-        pairs = [(j, j ^ bit) for j in range(size)]
-        length = value.shape[0] // 2
-        mine = lax.dynamic_slice_in_dim(value, side * length, length, 0)
-        other = lax.dynamic_slice_in_dim(value, (1 - side) * length, length, 0)
-        value = mine + lax.ppermute(other, axis, pairs)
-        taken.append((axis, pairs, side))
-    for axis, bit in whole:
-        pairs = [(j, j ^ bit) for j in range(lax.axis_size(axis))]
-        value = value + lax.ppermute(value, axis, pairs)
-    value = value * scale
-    for axis, pairs, side in reversed(taken):
-        other = lax.ppermute(value, axis, pairs)
-        value = jnp.where(
-            side == 0, jnp.concatenate([value, other], 0), jnp.concatenate([other, value], 0)
+def exchanged(values, axis, bit):
+    pairs = [(j, j ^ bit) for j in range(lax.axis_size(axis))]
+    return [lax.ppermute(value, axis, pairs) for value in values]
+
+
+def sum_over_devices(value, first, halved, whole, scale, meanwhile):
+    def side(axis, bit):
+        return lax.axis_index(axis) // bit % 2
+
+    def split(v, axis, bit):
+        length = v.shape[0] // 2
+        s = side(axis, bit)
+        mine = lax.dynamic_slice_in_dim(v, s * length, length, 0)
+        other = lax.dynamic_slice_in_dim(v, (1 - s) * length, length, 0)
+        return mine + exchanged([other], axis, bit)[0]
+
+    def joined(v, axis, bit):
+        other = exchanged([v], axis, bit)[0]
+        return jnp.where(
+            side(axis, bit) == 0, jnp.concatenate([v, other], 0), jnp.concatenate([other, v], 0)
         )
-    return value
+
+    value = split(value, *first)
+    cut = value.shape[0] // 2
+    chains = [value[:cut], value[cut:]]
+    for step in range(len(halved[0])):
+        chains = [split(v, *halved[k][step]) for k, v in enumerate(chains)]
+    for step in range(len(whole[0])):
+        chains = [v + exchanged([v], *whole[k][step])[0] for k, v in enumerate(chains)]
+        if step == 0:
+            chains, meanwhile = lax.optimization_barrier((chains, meanwhile))
+    chains = [v * scale for v in chains]
+    for step in reversed(range(len(halved[0]))):
+        chains = [joined(v, *halved[k][step]) for k, v in enumerate(chains)]
+    return joined(jnp.concatenate(chains, 0), *first), meanwhile
 
 
 def shards(object_field, probe, raw_counts, resample_delta, tile_row, offsets):
@@ -344,12 +352,14 @@
         order, count[None], received[:, 0], received[:, 1], arrived, probe, forward, backward,
         resample, resample.T, [object_field] + around, half, tile,
     )
-    halved = (("row_2", 1), ("col", 1), ("col", 2))
-    whole = (("col", 4), ("row_1", 1), ("row_0", 1), ("row_0", 2))
-    probe_grad = sum_over_devices(
-        probe_total.reshape(-1, points), halved, whole, 1.0 / math.sqrt(frame_total)
-    ).reshape(probe.shape)
     inward = [to_neighbour(piece, step) for piece, step in zip(outer, AROUND)]
+    x, z = ("row_0", 1), ("col", 2)
+    rest = (("row_0", 2), ("col", 4), ("col", 1), ("row_1", 1))
+    probe_grad, inward = sum_over_devices(
+        probe_total.reshape(-1, points), ("row_2", 1), ((x, z), (z, x)), (rest, rest[1::-1] + rest[2:]),
+        1.0 / math.sqrt(frame_total), inward,
+    )
+    probe_grad = probe_grad.reshape(probe.shape)
     back = [inward[AROUND.index((-a, -b))] for a, b in AROUND]
     object_grad = merge(own, back, half)
     return (object_grad, probe_grad)

time: 299 us -> 266 us (0.89)
  waiting for transfers between devices: 102 us -> 54.6 us
  starting transfers between devices: 119 us -> 162 us
  Pallas kernels: 58.1 us -> 27.9 us
    ppermute x10 -> x18, starting transfers between devices: 56.6 us -> 95.7 us  [exchanged(): return [lax.ppermute(value, axis, pairs) for value in values]]
    ppermute x16, waiting for transfers between devices: 60.7 us -> 33.3 us  [to_neighbour(): return lax.ppermute(value, ROW_COL, pairs)]
    pallas_call x1, Pallas kernels: 25.6 us -> 4.86 us  [spread(): pl.pallas_call(spread_kernel, grid_spec=pltpu.PrefetchScalarGridSpec(num_...]
    ppermute x10 -> x18, waiting for transfers between devices: 41.3 us -> 21.3 us  [exchanged(): return [lax.ppermute(value, axis, pairs) for value in values]]
    pallas_call x1, Pallas kernels: 29.1 us -> 19.7 us  [run_frames(): pl.pallas_call(functools.partial(frames_kernel, points=n, modes=modes, sp...]
    ppermute x16, starting transfers between devices: 48.8 us -> 52.3 us  [to_neighbour(): return lax.ppermute(value, ROW_COL, pairs)]
  transfers between devices with their start and end apart: 28 -> 36, of which waited for: 15 -> 15; matrix products, arithmetic and copies ran while one was open for 3% -> 4% of each run, Pallas kernels for 10% -> 3%
where the time goes in v2:
time: 266 us; the launch traced here: 263 us
  starting transfers between devices  162 us (61%)
  waiting for transfers between devices  54.6 us (21%)
  Pallas kernels  27.9 us (10%)
  local copies, waits for them, and re-layouts  8.59 us (3%)
  other arithmetic  8.42 us (3%)
    ppermute x18, starting transfers between devices, exchanged(): return [lax.ppermute(value, axis, pairs) for value in values]  95.7 us
    ppermute x16, starting transfers between devices, to_neighbour(): return lax.ppermute(value, ROW_COL, pairs)  52.3 us
    ppermute x16, waiting for transfers between devices, to_neighbour(): return lax.ppermute(value, ROW_COL, pairs)  33.3 us
    ppermute x18, waiting for transfers between devices, exchanged(): return [lax.ppermute(value, axis, pairs) for value in values]  21.3 us
    pallas_call x1, Pallas kernels, run_frames(): pl.pallas_call(functools.partial(frames_kernel, points=n, modes=modes, sp...  19.7 us
    all_to_all x1, starting transfers between devices, shards(): lax.all_to_all(requests, ROW, split_axis=0, concat_axis=0, tiled=True)  8.45 us
    all_to_all x1, starting transfers between devices, shards(): lax.all_to_all(slots, ROW, split_axis=0, concat_axis=0, tiled=True)  5.44 us
  transfers between devices with their start and end apart: 36, of which 15 were waited for; matrix products, arithmetic and copies ran while one was open for 4% of the time, Pallas kernels for 3%

profile of v2, /device:TPU:1, one launch (start us, length us, event | category | flops | bytes accessed | tf_op | source)
XLA Modules:
  0.0 263.3 jit_solution(12876464774286857510)
XLA Ops:
  2.8 8.4 %all-to-all-start = ((s32[16,1,3]{2,1,0:T(1,128)}), s32[16,1,3]{2,1,0:T(1,128)S(1)}, u32[]{:S(2)}, u32[]{:S(2)}) async-start(s32[16,1,3]{2,1,0:T(1,128)} %copy.14), calls=%async_computation | async-start | bytes 16384 | tf_op jit(solution)/shard_map/all_to_all | solution.py:340
  13.2 4.9 %collective-permute-start = (f32[2,128,128]{2,1,0:T(8,128)}, f32[2,128,128]{2,1,0:T(8,128)S(1)}, u32[]{:S(2)}, u32[]{:S(2)}) collective-permute-start(f32[2,128,128]{2,1,0:T(8,128)} %get-tuple-element.48), channel_id=1, source_target_pairs={{0,9},{1,10},{2,11},{3,12},{4,13},{5,14},{6,15},{8,17},{9,18},{10,... | collective-permute-start | bytes 393224 | tf_op jit(solution)/shard_map/ppermute | solution.py:251
  18.1 4.9 %spread.1 = bf16[16,256,256]{2,1,0:T(8,128)(2,1)} custom-call(s32[6]{0:T(128)} %bitcast.30, bf16[6,256,256]{2,1,0:T(8,128)(2,1)} %frame.1), custom_call_target="tpu_custom_call" | custom-call | tf_op jit(solution)/shard_map/spread/pallas_call | solution.py:40
  22.9 5.4 %all-to-all-start.1 = ((bf16[16,256,256]{2,1,0:T(8,128)(2,1)}), bf16[16,256,256]{2,1,0:T(8,128)(2,1)}, u32[]{:S(2)}, u32[]{:S(2)}) async-start(bf16[16,256,256]{2,1,0:T(8,128)(2,1)} %spread.1), calls=%async_computation.1 | async-start | bytes 4194304 | tf_op jit(solution)/shard_map/all_to_all | solution.py:341
  28.5 5.2 %collective-permute-start.1 = (f32[2,128,512]{2,1,0:T(8,128)S(1)}, f32[2,128,512]{2,1,0:T(8,128)}, u32[]{:S(2)}, u32[]{:S(2)}) collective-permute-start(f32[2,128,512]{2,1,0:T(8,128)S(1)} %get-tuple-element.50), channel_id=1, source_target_pairs={{0,8},{1,9},{2,10},{3,11},{4,12},{5,13},{6,14},{7,15},{8,16},{9,17... | collective-permute-start | bytes 1572872 | tf_op jit(solution)/shard_map/ppermute | solution.py:251
  36.0 4.0 %collective-permute-start.3 = (f32[2,512,128]{2,1,0:T(8,128)}, f32[2,512,128]{2,1,0:T(8,128)S(1)}, u32[]{:S(2)}, u32[]{:S(2)}) collective-permute-start(f32[2,512,128]{2,1,0:T(8,128)} %get-tuple-element.52), channel_id=1, source_target_pairs={{0,1},{1,2},{2,3},{3,4},{4,5},{5,6},{6,7},{8,9},{9,10},{10,11},{11... | collective-permute-start | bytes 1572872 | tf_op jit(solution)/shard_map/ppermute | solution.py:251
  47.5 6.1 %collective-permute-start.5 = (f32[2,128,128]{2,1,0:T(8,128)S(1)}, f32[2,128,128]{2,1,0:T(8,128)S(1)}, u32[]{:S(2)}, u32[]{:S(2)}) collective-permute-start(f32[2,128,128]{2,1,0:T(8,128)S(1)} %copy-done.12), channel_id=1, source_target_pairs={{8,1},{9,2},{10,3},{11,4},{12,5},{13,6},{14,7},{16,9},{17,10},{18,... | collective-permute-start | bytes 393224 | tf_op jit(solution)/shard_map/ppermute | solution.py:251
  56.3 20.4 %collective-permute-done.5.refs_6_ = f32[2,128,128]{2,1,0:T(8,128)S(1)} collective-permute-done((f32[2,128,128]{2,1,0:T(8,128)S(1)}, f32[2,128,128]{2,1,0:T(8,128)S(1)}, u32[]{:S(2)}, u32[]{:S(2)}) %collective-permute-start.5) | collective-permute-done | bytes 131104 | tf_op jit(solution)/shard_map/ppermute | solution.py:251
  78.7 5.5 %collective-permute-done.7.refs_8_ = f32[2,128,128]{2,1,0:T(8,128)S(1)} collective-permute-done((f32[2,128,128]{2,1,0:T(8,128)S(1)}, f32[2,128,128]{2,1,0:T(8,128)S(1)}, u32[]{:S(2)}, u32[]{:S(2)}) %collective-permute-start.7) | collective-permute-done | bytes 131104 | tf_op jit(solution)/shard_map/ppermute | solution.py:251
  84.2 5.3 %collective-permute-done.4.refs_5_ = f32[2,512,128]{2,1,0:T(8,128)S(1)} collective-permute-done((f32[2,512,128]{2,1,0:T(8,128)}, f32[2,512,128]{2,1,0:T(8,128)S(1)}, u32[]{:S(2)}, u32[]{:S(2)}) %collective-permute-start.4) | collective-permute-done | bytes 524320 | tf_op jit(solution)/shard_map/ppermute | solution.py:251
  90.5 19.7 %frames.1 = (f32[3,2,256,256]{3,2,1,0:T(8,128)}, f32[2,512,512]{2,1,0:T(8,128)}, f32[2,128,128]{2,1,0:T(8,128)}, f32[2,128,512]{2,1,0:T(8,128)}, f32[2,128,128]{...) custom-call(s32[16]{0:T(128)} %select_reduce_fusion.order, ...), custom_call_target="tpu_custom_call" | custom-call | tf_op jit(solution)/shard_map/frames/pallas_call | solution.py:232
  111.5 15.5 %collective-permute-start.8 = (f32[768,256]{1,0:T(8,128)S(1)}, f32[768,256]{1,0:T(8,128)S(1)}, u32[]{:S(2)}, u32[]{:S(2)}) collective-permute-start(f32[768,256]{1,0:T(8,128)S(1)} %constant_dynamic-slice_fusion.4), channel_id=1, source_target_pairs={{0,8},{8,0},{1,9},{9,1},{2,10},{10,2},{3,11},{11,3},{4,12},{12,4},... | collective-permute-start | bytes 2359304 | tf_op jit(solution)/shard_map/ppermute | solution.py:292
  133.5 3.7 %collective-permute-start.17 = (f32[2,128,128]{2,1,0:T(8,128)}, f32[2,128,128]{2,1,0:T(8,128)S(1)}, u32[]{:S(2)}, u32[]{:S(2)}) collective-permute-start(f32[2,128,128]{2,1,0:T(8,128)} %get-tuple-element.26), channel_id=1, source_target_pairs={{8,1},{9,2},{10,3},{11,4},{12,5},{13,6},{14,7},{16,9},{17,10},{18,... | collective-permute-start | bytes 393224 | tf_op jit(solution)/shard_map/ppermute | solution.py:251
  138.6 36.4 %collective-permute-start.12 = (f32[192,256]{1,0:T(8,128)S(1)}, f32[192,256]{1,0:T(8,128)S(1)}, u32[]{:S(2)}, u32[]{:S(2)}) collective-permute-start(f32[192,256]{1,0:T(8,128)S(1)} %constant_dynamic-slice_fusion.1), channel_id=1, source_target_pairs={{0,2},{1,3},{2,0},{3,1},{4,6},{5,7},{6,4},{7,5},{8,10},{9,11},{10,... | collective-permute-start | bytes 589832 | tf_op jit(solution)/shard_map/ppermute | solution.py:292
  180.9 4.8 %collective-permute-start.19 = (f32[2,512,128]{2,1,0:T(8,128)}, f32[2,512,128]{2,1,0:T(8,128)}, u32[]{:S(2)}, u32[]{:S(2)}) collective-permute-start(f32[2,512,128]{2,1,0:T(8,128)} %get-tuple-element.28), channel_id=1, source_target_pairs={{0,1},{1,2},{2,3},{3,4},{4,5},{5,6},{6,7},{8,9},{9,10},{10,11},{11... | collective-permute-start | bytes 1572872 | tf_op jit(solution)/shard_map/ppermute | solution.py:251
  185.7 6.4 %collective-permute-start.21 = (f32[2,128,512]{2,1,0:T(8,128)S(1)}, f32[2,128,512]{2,1,0:T(8,128)}, u32[]{:S(2)}, u32[]{:S(2)}) collective-permute-start(f32[2,128,512]{2,1,0:T(8,128)S(1)} %copy-done.17), channel_id=1, source_target_pairs={{0,8},{1,9},{2,10},{3,11},{4,12},{5,13},{6,14},{7,15},{8,16},{9,17... | collective-permute-start | bytes 1572872 | tf_op jit(solution)/shard_map/ppermute | solution.py:251
  192.2 4.6 %collective-permute-start.13 = (f32[96,256]{1,0:T(8,128)S(1)}, f32[96,256]{1,0:T(8,128)S(1)}, u32[]{:S(2)}, u32[]{:S(2)}) collective-permute-start(f32[96,256]{1,0:T(8,128)S(1)} %constant_dynamic-slice_fusion), channel_id=1, source_target_pairs={{0,32},{32,0},{64,96},{96,64},{1,33},{33,1},{65,97},{97,65},{2,34}... | collective-permute-start | bytes 294920 | tf_op jit(solution)/shard_map/ppermute | solution.py:292
  199.9 4.8 %collective-permute-done.11 = f32[96,256]{1,0:T(8,128)S(1)} collective-permute-done((f32[96,256]{1,0:T(8,128)S(1)}, f32[96,256]{1,0:T(8,128)S(1)}, u32[]{:S(2)}, u32[]{:S(2)}) %collective-permute-start.11) | collective-permute-done | bytes 98336 | tf_op jit(solution)/shard_map/ppermute | solution.py:292
  209.7 5.2 %collective-permute-start.22 = (f32[2,128,128]{2,1,0:T(8,128)}, f32[2,128,128]{2,1,0:T(8,128)S(1)}, u32[]{:S(2)}, u32[]{:S(2)}) collective-permute-start(f32[2,128,128]{2,1,0:T(8,128)} %get-tuple-element.31), channel_id=1, source_target_pairs={{0,9},{1,10},{2,11},{3,12},{4,13},{5,14},{6,15},{8,17},{9,18},{10,... | collective-permute-start | bytes 393224 | tf_op jit(solution)/shard_map/ppermute | solution.py:251
  217.2 6.8 %collective-permute-start.28 = (f32[96,256]{1,0:T(8,128)S(1)}, f32[96,256]{1,0:T(8,128)S(1)}, u32[]{:S(2)}, u32[]{:S(2)}) collective-permute-start(f32[96,256]{1,0:T(8,128)S(1)} %add.134), channel_id=1, source_target_pairs={{0,64},{32,96},{64,0},{96,32},{1,65},{33,97},{65,1},{97,33},{2,66}... | collective-permute-start | bytes 294920 | tf_op jit(solution)/shard_map/ppermute | solution.py:292
  224.0 3.2 %collective-permute-start.23 = (f32[96,256]{1,0:T(8,128)S(1)}, f32[96,256]{1,0:T(8,128)S(1)}, u32[]{:S(2)}, u32[]{:S(2)}) collective-permute-start(f32[96,256]{1,0:T(8,128)S(1)} %add.127), channel_id=1, source_target_pairs={{0,4},{1,5},{2,6},{3,7},{4,0},{5,1},{6,2},{7,3},{8,12},{9,13},{10,... | collective-permute-start | bytes 294920 | tf_op jit(solution)/shard_map/ppermute | solution.py:292
  236.6 5.8 %collective-permute-start.31 = (f32[96,256]{1,0:T(8,128)S(1)}, f32[96,256]{1,0:T(8,128)S(1)}, u32[]{:S(2)}, u32[]{:S(2)}) collective-permute-start(f32[96,256]{1,0:T(8,128)S(1)} %add_multiply_fusion), channel_id=1, source_target_pairs={{0,32},{32,0},{64,96},{96,64},{1,33},{33,1},{65,97},{97,65},{2,34}... | collective-permute-start | bytes 294920 | tf_op jit(solution)/shard_map/ppermute | solution.py:292
  252.3 6.2 %collective-permute-start.33 = (f32[768,256]{1,0:T(8,128)S(1)}, f32[768,256]{1,0:T(8,128)S(1)}, u32[]{:S(2)}, u32[]{:S(2)}) collective-permute-start(f32[768,256]{1,0:T(8,128)S(1)} %pad_maximum_fusion), channel_id=1, source_target_pairs={{0,8},{8,0},{1,9},{9,1},{2,10},{10,2},{3,11},{11,3},{4,12},{12,4},... | collective-permute-start | bytes 2359304 | tf_op jit(solution)/shard_map/ppermute | solution.py:292
  258.6 3.4 %merge.1 = f32[2,512,512]{2,1,0:T(8,128)} custom-call(f32[2,512,512]{2,1,0:T(8,128)} %get-tuple-element.22.own, f32[2,128,128]{2,1,0:T(8,128)} %copy-done.16, f32[2,128,512]{2,1,0:T(8,128)} %collective-permute-done.21.refs_1_, f32[2,128,128]{2,1,0:T(8,128)} %copy-done.15, f32[2,512,128]{2,1,0:T(8,128)} %collective-permute-done.19.refs_3_, ...), custom_call_target="tpu_custom_call" | custom-call | tf_op jit(solution)/shard_map/merge/pallas_call | solution.py:277
  (134 shorter events, 64.7 us)
Async XLA Ops:
  2.8 20.1 %all-to-all-start = ((s32[16,1,3]{2,1,0:T(1,128)}), s32[16,1,3]{2,1,0:T(1,128)S(1)}, u32[]{:S(2)}, u32[]{:S(2)}) async-start(s32[16,1,3]{2,1,0:T(1,128)} %copy.14), calls=%async_computation | async-start | bytes 16384 | tf_op jit(solution)/shard_map/all_to_all | solution.py:340
  13.2 34.3 %collective-permute-start = (f32[2,128,128]{2,1,0:T(8,128)}, f32[2,128,128]{2,1,0:T(8,128)S(1)}, u32[]{:S(2)}, u32[]{:S(2)}) collective-permute-start(f32[2,128,128]{2,1,0:T(8,128)} %get-tuple-element.48), channel_id=1, source_target_pairs={{0,9},{1,10},{2,11},{3,12},{4,13},{5,14},{6,15},{8,17},{9,18},{10,... | collective-permute-start | bytes 393224 | tf_op jit(solution)/shard_map/ppermute | solution.py:251
  22.9 66.5 %all-to-all-start.1 = ((bf16[16,256,256]{2,1,0:T(8,128)(2,1)}), bf16[16,256,256]{2,1,0:T(8,128)(2,1)}, u32[]{:S(2)}, u32[]{:S(2)}) async-start(bf16[16,256,256]{2,1,0:T(8,128)(2,1)} %spread.1), calls=%async_computation.1 | async-start | bytes 4194304 | tf_op jit(solution)/shard_map/all_to_all | solution.py:341
  28.5 55.7 %collective-permute-start.1 = (f32[2,128,512]{2,1,0:T(8,128)S(1)}, f32[2,128,512]{2,1,0:T(8,128)}, u32[]{:S(2)}, u32[]{:S(2)}) collective-permute-start(f32[2,128,512]{2,1,0:T(8,128)S(1)} %get-tuple-element.50), channel_id=1, source_target_pairs={{0,8},{1,9},{2,10},{3,11},{4,12},{5,13},{6,14},{7,15},{8,16},{9,17... | collective-permute-start | bytes 1572872 | tf_op jit(solution)/shard_map/ppermute | solution.py:251
  33.6 19.9 %collective-permute-start.2 = (f32[2,128,128]{2,1,0:T(8,128)}, f32[2,128,128]{2,1,0:T(8,128)}, u32[]{:S(2)}, u32[]{:S(2)}) collective-permute-start(f32[2,128,128]{2,1,0:T(8,128)} %get-tuple-element.47), channel_id=1, source_target_pairs={{1,8},{2,9},{3,10},{4,11},{5,12},{6,13},{7,14},{9,16},{10,17},{11,... | collective-permute-start | bytes 393224 | tf_op jit(solution)/shard_map/ppermute | solution.py:251
  36.0 48.2 %collective-permute-start.3 = (f32[2,512,128]{2,1,0:T(8,128)}, f32[2,512,128]{2,1,0:T(8,128)S(1)}, u32[]{:S(2)}, u32[]{:S(2)}) collective-permute-start(f32[2,512,128]{2,1,0:T(8,128)} %get-tuple-element.52), channel_id=1, source_target_pairs={{0,1},{1,2},{2,3},{3,4},{4,5},{5,6},{6,7},{8,9},{9,10},{10,11},{11... | collective-permute-start | bytes 1572872 | tf_op jit(solution)/shard_map/ppermute | solution.py:251
  40.0 49.4 %collective-permute-start.4 = (f32[2,512,128]{2,1,0:T(8,128)}, f32[2,512,128]{2,1,0:T(8,128)S(1)}, u32[]{:S(2)}, u32[]{:S(2)}) collective-permute-start(f32[2,512,128]{2,1,0:T(8,128)} %get-tuple-element.51), channel_id=1, source_target_pairs={{1,0},{2,1},{3,2},{4,3},{5,4},{6,5},{7,6},{9,8},{10,9},{11,10},{12... | collective-permute-start | bytes 1572872 | tf_op jit(solution)/shard_map/ppermute | solution.py:251
  47.5 29.1 %collective-permute-start.5 = (f32[2,128,128]{2,1,0:T(8,128)S(1)}, f32[2,128,128]{2,1,0:T(8,128)S(1)}, u32[]{:S(2)}, u32[]{:S(2)}) collective-permute-start(f32[2,128,128]{2,1,0:T(8,128)S(1)} %copy-done.12), channel_id=1, source_target_pairs={{8,1},{9,2},{10,3},{11,4},{12,5},{13,6},{14,7},{16,9},{17,10},{18,... | collective-permute-start | bytes 393224 | tf_op jit(solution)/shard_map/ppermute | solution.py:251
  53.6 35.8 %collective-permute-start.6 = (f32[2,128,512]{2,1,0:T(8,128)S(1)}, f32[2,128,512]{2,1,0:T(8,128)S(1)}, u32[]{:S(2)}, u32[]{:S(2)}) collective-permute-start(f32[2,128,512]{2,1,0:T(8,128)S(1)} %get-tuple-element.49), channel_id=1, source_target_pairs={{8,0},{9,1},{10,2},{11,3},{12,4},{13,5},{14,6},{15,7},{16,8},{17,9... | collective-permute-start | bytes 1572872 | tf_op jit(solution)/shard_map/ppermute | solution.py:251
  111.5 17.4 %collective-permute-start.8 = (f32[768,256]{1,0:T(8,128)S(1)}, f32[768,256]{1,0:T(8,128)S(1)}, u32[]{:S(2)}, u32[]{:S(2)}) collective-permute-start(f32[768,256]{1,0:T(8,128)S(1)} %constant_dynamic-slice_fusion.4), channel_id=1, source_target_pairs={{0,8},{8,0},{1,9},{9,1},{2,10},{10,2},{3,11},{11,3},{4,12},{12,4},... | collective-permute-start | bytes 2359304 | tf_op jit(solution)/shard_map/ppermute | solution.py:292
  129.1 9.5 %collective-permute-start.9 = (f32[192,256]{1,0:T(8,128)S(1)}, f32[192,256]{1,0:T(8,128)S(1)}, u32[]{:S(2)}, u32[]{:S(2)}) collective-permute-start(f32[192,256]{1,0:T(8,128)S(1)} %constant_dynamic-slice_fusion.3), channel_id=1, source_target_pairs={{0,32},{32,0},{64,96},{96,64},{1,33},{33,1},{65,97},{97,65},{2,34}... | collective-permute-start | bytes 589832 | tf_op jit(solution)/shard_map/ppermute | solution.py:292
  129.9 49.7 %collective-permute-start.15 = (f32[2,128,128]{2,1,0:T(8,128)S(1)}, f32[2,128,128]{2,1,0:T(8,128)S(1)}, u32[]{:S(2)}, u32[]{:S(2)}) collective-permute-start(f32[2,128,128]{2,1,0:T(8,128)S(1)} %copy-done.18), channel_id=1, source_target_pairs={{9,0},{10,1},{11,2},{12,3},{13,4},{14,5},{15,6},{17,8},{18,9},{19,... | collective-permute-start | bytes 393224 | tf_op jit(solution)/shard_map/ppermute | solution.py:251
  131.2 85.9 %collective-permute-start.16 = (f32[2,128,512]{2,1,0:T(8,128)}, f32[2,128,512]{2,1,0:T(8,128)S(1)}, u32[]{:S(2)}, u32[]{:S(2)}) collective-permute-start(f32[2,128,512]{2,1,0:T(8,128)} %get-tuple-element.25), channel_id=1, source_target_pairs={{8,0},{9,1},{10,2},{11,3},{12,4},{13,5},{14,6},{15,7},{16,8},{17,9... | collective-permute-start | bytes 1572872 | tf_op jit(solution)/shard_map/ppermute | solution.py:251
  133.5 47.4 %collective-permute-start.17 = (f32[2,128,128]{2,1,0:T(8,128)}, f32[2,128,128]{2,1,0:T(8,128)S(1)}, u32[]{:S(2)}, u32[]{:S(2)}) collective-permute-start(f32[2,128,128]{2,1,0:T(8,128)} %get-tuple-element.26), channel_id=1, source_target_pairs={{8,1},{9,2},{10,3},{11,4},{12,5},{13,6},{14,7},{16,9},{17,10},{18,... | collective-permute-start | bytes 393224 | tf_op jit(solution)/shard_map/ppermute | solution.py:251
  137.2 48.5 %collective-permute-start.20 = (f32[2,128,128]{2,1,0:T(8,128)}, f32[2,128,128]{2,1,0:T(8,128)S(1)}, u32[]{:S(2)}, u32[]{:S(2)}) collective-permute-start(f32[2,128,128]{2,1,0:T(8,128)} %get-tuple-element.29), channel_id=1, source_target_pairs={{1,8},{2,9},{3,10},{4,11},{5,12},{6,13},{7,14},{9,16},{10,17},{11,... | collective-permute-start | bytes 393224 | tf_op jit(solution)/shard_map/ppermute | solution.py:251
  138.6 39.5 %collective-permute-start.12 = (f32[192,256]{1,0:T(8,128)S(1)}, f32[192,256]{1,0:T(8,128)S(1)}, u32[]{:S(2)}, u32[]{:S(2)}) collective-permute-start(f32[192,256]{1,0:T(8,128)S(1)} %constant_dynamic-slice_fusion.1), channel_id=1, source_target_pairs={{0,2},{1,3},{2,0},{3,1},{4,6},{5,7},{6,4},{7,5},{8,10},{9,11},{10,... | collective-permute-start | bytes 589832 | tf_op jit(solution)/shard_map/ppermute | solution.py:292
  178.1 14.1 %collective-permute-start.10 = (f32[96,256]{1,0:T(8,128)S(1)}, f32[96,256]{1,0:T(8,128)S(1)}, u32[]{:S(2)}, u32[]{:S(2)}) collective-permute-start(f32[96,256]{1,0:T(8,128)S(1)} %constant_dynamic-slice_fusion.2), channel_id=1, source_target_pairs={{0,2},{1,3},{2,0},{3,1},{4,6},{5,7},{6,4},{7,5},{8,10},{9,11},{10,... | collective-permute-start | bytes 294920 | tf_op jit(solution)/shard_map/ppermute | solution.py:292
  179.6 37.5 %collective-permute-start.18 = (f32[2,512,128]{2,1,0:T(8,128)}, f32[2,512,128]{2,1,0:T(8,128)S(1)}, u32[]{:S(2)}, u32[]{:S(2)}) collective-permute-start(f32[2,512,128]{2,1,0:T(8,128)} %get-tuple-element.27), channel_id=1, source_target_pairs={{1,0},{2,1},{3,2},{4,3},{5,4},{6,5},{7,6},{9,8},{10,9},{11,10},{12... | collective-permute-start | bytes 1572872 | tf_op jit(solution)/shard_map/ppermute | solution.py:251
  180.9 36.2 %collective-permute-start.19 = (f32[2,512,128]{2,1,0:T(8,128)}, f32[2,512,128]{2,1,0:T(8,128)}, u32[]{:S(2)}, u32[]{:S(2)}) collective-permute-start(f32[2,512,128]{2,1,0:T(8,128)} %get-tuple-element.28), channel_id=1, source_target_pairs={{0,1},{1,2},{2,3},{3,4},{4,5},{5,6},{6,7},{8,9},{9,10},{10,11},{11... | collective-permute-start | bytes 1572872 | tf_op jit(solution)/shard_map/ppermute | solution.py:251
  185.7 31.4 %collective-permute-start.21 = (f32[2,128,512]{2,1,0:T(8,128)S(1)}, f32[2,128,512]{2,1,0:T(8,128)}, u32[]{:S(2)}, u32[]{:S(2)}) collective-permute-start(f32[2,128,512]{2,1,0:T(8,128)S(1)} %copy-done.17), channel_id=1, source_target_pairs={{0,8},{1,9},{2,10},{3,11},{4,12},{5,13},{6,14},{7,15},{8,16},{9,17... | collective-permute-start | bytes 1572872 | tf_op jit(solution)/shard_map/ppermute | solution.py:251
  217.2 10.0 %collective-permute-start.28 = (f32[96,256]{1,0:T(8,128)S(1)}, f32[96,256]{1,0:T(8,128)S(1)}, u32[]{:S(2)}, u32[]{:S(2)}) collective-permute-start(f32[96,256]{1,0:T(8,128)S(1)} %add.134), channel_id=1, source_target_pairs={{0,64},{32,96},{64,0},{96,32},{1,65},{33,97},{65,1},{97,33},{2,66}... | collective-permute-start | bytes 294920 | tf_op jit(solution)/shard_map/ppermute | solution.py:292
  233.8 8.6 %collective-permute-start.25 = (f32[96,256]{1,0:T(8,128)S(1)}, f32[96,256]{1,0:T(8,128)S(1)}, u32[]{:S(2)}, u32[]{:S(2)}) collective-permute-start(f32[96,256]{1,0:T(8,128)S(1)} %add.136), channel_id=1, source_target_pairs={{0,16},{16,0},{1,17},{17,1},{2,18},{18,2},{3,19},{19,3},{4,20},{20... | collective-permute-start | bytes 294920 | tf_op jit(solution)/shard_map/ppermute | solution.py:292
  236.6 8.2 %collective-permute-start.31 = (f32[96,256]{1,0:T(8,128)S(1)}, f32[96,256]{1,0:T(8,128)S(1)}, u32[]{:S(2)}, u32[]{:S(2)}) collective-permute-start(f32[96,256]{1,0:T(8,128)S(1)} %add_multiply_fusion), channel_id=1, source_target_pairs={{0,32},{32,0},{64,96},{96,64},{1,33},{33,1},{65,97},{97,65},{2,34}... | collective-permute-start | bytes 294920 | tf_op jit(solution)/shard_map/ppermute | solution.py:292
  252.3 9.7 %collective-permute-start.33 = (f32[768,256]{1,0:T(8,128)S(1)}, f32[768,256]{1,0:T(8,128)S(1)}, u32[]{:S(2)}, u32[]{:S(2)}) collective-permute-start(f32[768,256]{1,0:T(8,128)S(1)} %pad_maximum_fusion), channel_id=1, source_target_pairs={{0,8},{8,0},{1,9},{9,1},{2,10},{10,2},{3,11},{11,3},{4,12},{12,4},... | collective-permute-start | bytes 2359304 | tf_op jit(solution)/shard_map/ppermute | solution.py:292
  (31 other events, 537.1 us)

commit v3 on v1

v3 whole, which is shorter than its diff:
```python
import functools
import math

import jax
import jax.numpy as jnp
from jax import lax
from jax.experimental import pallas as pl
from jax.experimental.pallas import tpu as pltpu
from jax.sharding import Mesh
from jax.sharding import PartitionSpec as P

ROW = ("x", "y_far", "core")
COL = ("z", "y_near")
ROW_COL = ROW + COL
VMEM_BYTES = 52 * 2**20
HEADROOM = 14.0
NOTE_ROWS = 16


def dft_table(left, right, points, sign):
    phases = left[:, None] * right[None, :] % points
    angles = phases.astype(jnp.float32) * (2.0 * math.pi / points)
    norming = 1.0 / math.sqrt(points)
    cosine = jnp.cos(angles) * norming
    sine_part = -jnp.sin(angles) * norming * sign
    table = jnp.concatenate(
        [jnp.concatenate([cosine, -sine_part], 1), jnp.concatenate([sine_part, cosine], 1)], 0
    )
    return table.astype(jnp.bfloat16)


def spread_kernel(target, counts, slots, held, sems):
    count = counts.shape[0]
    inward = [pltpu.make_async_copy(counts.at[j], held.at[j], sems.at[0, j]) for j in range(count)]
    outward = [pltpu.make_async_copy(held.at[j], slots.at[target[j]], sems.at[1, j]) for j in range(count)]
    for copy in inward:
        copy.start()
    for j in range(count):
        inward[j].wait()
        outward[j].start()
    for copy in outward:
        copy.wait()


def spread(target, counts, slot_count):
    return pl.pallas_call(
        spread_kernel,
        grid_spec=pltpu.PrefetchScalarGridSpec(
            num_scalar_prefetch=1,
            grid=(1,),
            in_specs=[pl.BlockSpec(memory_space=pl.ANY)],
            out_specs=pl.BlockSpec(memory_space=pl.ANY),
            scratch_shapes=[
                pltpu.VMEM(counts.shape, counts.dtype),
                pltpu.SemaphoreType.DMA((2, counts.shape[0])),
            ],
        ),
        out_shape=jax.ShapeDtypeStruct((slot_count,) + counts.shape[1:], counts.dtype),
        name="spread",
    )(target, counts)


def parts_of(half, tile):
    end = half + tile
    return [
        [(0, half, half, tile, tile)],
        [(0, 0, half, half, tile)],
        [(0, end, half, half, tile)],
        [(0, half, 0, tile, half)],
        [(0, half, end, tile, half)],
        [(0, 0, 0, half, half), (half, end, 0, half, half)],
        [(0, 0, end, half, half), (half, end, end, half, half)],
    ]


def copies_of(arrays, parts, whole, sems):
    copies = []
    for array, spots in zip(arrays, parts):
        for first, r, c, h, w in spots:
            source = array.at[:, pl.ds(first, h), :]
            copies.append(
                pltpu.make_async_copy(source, whole.at[:, pl.ds(r, h), pl.ds(c, w)], sems.at[len(copies)])
            )
    return copies


def dot(x, y):
    return jnp.dot(x, y, preferred_element_type=jnp.float32)


def place_of(top, left):
    floor = pl.multiple_of(top // 8 * 8, 8)
    base = pl.multiple_of(left // 128 * 128, 128)
    return floor, base, top - floor, left - base


def waves_kernel(count, tops, lefts, probe_all, even_all, odd_all, *refs, points, modes, parts):
    pieces, (half_all, win_all, probe, even, odd, ext, stack, half_buffer, win_buffer, sems, out_sems) = (
        refs[: len(parts)], refs[len(parts) :]
    )
    n = points
    mid = n // 2
    tiles = n // 128
    copies = copies_of(pieces, parts, ext, sems)
    copies += [
        pltpu.make_async_copy(source, held, sems.at[len(copies) + k])
        for k, (source, held) in enumerate(((probe_all, probe), (even_all, even), (odd_all, odd)))
    ]
    for copy in copies:
        copy.start()
    for copy in copies:
        copy.wait()

    def leaving(i):
        slot = lax.rem(i, 2)
        return [
            pltpu.make_async_copy(half_buffer.at[slot], half_all.at[i], out_sems.at[slot, 0]),
            pltpu.make_async_copy(win_buffer.at[slot], win_all.at[i], out_sems.at[slot, 1]),
        ]

    def finish(i):
        @pl.when(i >= 0)
        def _():
            for copy in leaving(jnp.maximum(i, 0)):
                copy.wait()

    @pl.loop(0, count[0])
    def _(i):
        finish(i - 2)
        half_done = half_buffer.at[lax.rem(i, 2)]
        win = win_buffer.at[lax.rem(i, 2)]
        floor, base, low, shift = place_of(tops[i], lefts[i])
        back = lax.rem(128 - shift, 128)
        up = lax.rem(8 - low, 8)
        keep = lax.broadcasted_iota(jnp.int32, (8, 128), 1) < 128 - shift
        upper = lax.broadcasted_iota(jnp.int32, (8, 128), 0) < 8 - low

        def strip(part, g):
            cols = [
                pltpu.roll(ext[part, pl.ds(floor + 8 * g, 8), pl.ds(base + 128 * j, 128)], back, 1)
                for j in range(tiles + 1)
            ]
            vals = [jnp.where(keep, cols[j], cols[j + 1]) for j in range(tiles)]
            return [pltpu.roll(v, up, 0) for v in vals]

        for part in range(2):
            prev = strip(part, 0)
            for g in range(n // 8):
                following = strip(part, g + 1)
                for j in range(tiles):
                    win[part, j, 8 * g : 8 * g + 8, :] = jnp.where(
                        upper, prev[j], following[j]
                    )
                prev = following
        for parity in range(2):
            for r in range(0, mid, 16):
                o_re, o_im = [
                    jnp.concatenate(
                        [win[part, j, pl.ds(2 * r + parity, 16, stride=2), :] for j in range(tiles)], 1
                    )
                    for part in range(2)
                ]
                for m in range(modes):
                    p_re = probe[m, 0, parity, r : r + 16, :]
                    p_im = probe[m, 1, parity, r : r + 16, :]
                    psi_re = (p_re * o_re - p_im * o_im).astype(jnp.bfloat16)
                    psi_im = (p_re * o_im + p_im * o_re).astype(jnp.bfloat16)
                    stack[parity, r : r + 16, m * n : (m + 1) * n] = psi_re
                    stack[parity, mid + r : mid + r + 16, m * n : (m + 1) * n] = psi_im
        for m in range(modes):
            e = dot(even[...], stack[0, :, m * n : (m + 1) * n])
            o = dot(odd[...], stack[1, :, m * n : (m + 1) * n])
            for k, both in enumerate(((e + o).astype(jnp.bfloat16), (e - o).astype(jnp.bfloat16))):
                r = m * n + k * mid
                half_done[r : r + mid, 0:n] = both[:mid]
                half_done[r : r + mid, n : 2 * n] = both[mid:]
        for copy in leaving(i):
            copy.start()

    finish(count[0] - 2)
    finish(count[0] - 1)


def frames_kernel(
    order, count, tops, lefts, raw_all, half_all, win_all,
    probe_all, turn_all, row_even_all, row_odd_all, col_even_all, col_odd_all, res_all, res_t_all,
    pgrad, grad, probe, turn, row_even, row_odd, col_even, col_odd, res, res_t,
    raw_buffer, half_buffer, win_buffer, field, rows, stack, update, amp, sems, const_sems, *, points, modes,
):
    n = points
    mid, quarter = n // 2, n // 4
    tiles = n // 128

    def arriving(i):
        slot = lax.rem(i, 2)
        return [
            pltpu.make_async_copy(half_all.at[i], half_buffer.at[slot], sems.at[slot, 0]),
            pltpu.make_async_copy(raw_all.at[order[i]], raw_buffer.at[slot], sems.at[slot, 1]),
            pltpu.make_async_copy(win_all.at[i], win_buffer.at[slot], sems.at[slot, 2]),
        ]

    def fetch(i):
        @pl.when(i < count[0])
        def _():
            for copy in arriving(i):
                copy.start()

    fetch(0)
    sources = (probe_all, turn_all, row_even_all, row_odd_all, col_even_all, col_odd_all, res_all, res_t_all)
    held = (probe, turn, row_even, row_odd, col_even, col_odd, res, res_t)
    copies = [pltpu.make_async_copy(a, b, const_sems.at[k]) for k, (a, b) in enumerate(zip(sources, held))]
    for copy in copies:
        copy.start()
    grad[...] = jnp.zeros(grad.shape, jnp.float32)
    pgrad[...] = jnp.zeros(pgrad.shape, jnp.float32)
    for copy in copies:
        copy.wait()

    @pl.loop(0, count[0])
    def _(i):
        for copy in arriving(i):
            copy.wait()
        fetch(i + 1)
        slot = lax.rem(i, 2)
        half_done, raw, win = half_buffer.at[slot], raw_buffer.at[slot], win_buffer.at[slot]
        floor, base, low, shift = place_of(tops[i], lefts[i])
        field[...] = dot(half_done[...], turn[...])
        first = dot(res[...], raw[...]).astype(jnp.bfloat16)
        second = dot(first, res_t[...])
        amp[...] = jnp.sqrt(jnp.maximum(second, 0.0)).astype(jnp.bfloat16).astype(jnp.float32)
        for r in range(0, n, 16):
            far = [field[m * n + r : m * n + r + 16, :] for m in range(modes)]
            total = far[0] * far[0]
            for m in range(1, modes):
                total = total + far[m] * far[m]
            scaling = []
            for k in range(2):
                intensity = total[:, 2 * k * mid : (2 * k + 1) * mid] + total[:, (2 * k + 1) * mid : (2 * k + 2) * mid]
                s = 1.0 - amp[r : r + 16, k * mid : (k + 1) * mid] * lax.rsqrt(jnp.maximum(intensity, 1.0))
                scaling += [s, s]
            scaling = jnp.concatenate(scaling, 1)
            for m in range(modes):
                rows[m * n + r : m * n + r + 16, :] = (far[m] * scaling).astype(jnp.bfloat16)
        for m in range(modes):
            e = dot(rows[m * n : (m + 1) * n, 0:n], row_even[...])
            o = dot(rows[m * n : (m + 1) * n, n : 2 * n], row_odd[...])
            for k, both in enumerate(((e + o).astype(jnp.bfloat16), (e - o).astype(jnp.bfloat16))):
                c = m * n + k * mid
                for part in range(2):
                    for block in range(4):
                        r = part * mid + block // 2 * quarter
                        stack[block % 2, r : r + quarter, c : c + mid] = both[
                            block * quarter : (block + 1) * quarter, part * mid : (part + 1) * mid
                        ]
        for m in range(modes):
            c = m * n
            e = dot(col_even[...], stack[0, :, c : c + n])
            o = dot(col_odd[...], stack[1, :, c : c + n])
            for k, both in enumerate((e + o, e - o)):
                update[k * mid : (k + 1) * mid, c : c + n] = both[:mid]
                update[n + k * mid : n + (k + 1) * mid, c : c + n] = both[mid:]
        fresh = lax.broadcasted_iota(jnp.int32, (8, 128), 1) >= shift
        lower = lax.broadcasted_iota(jnp.int32, (8, 128), 0) >= low
        zero = jnp.zeros((8, 128), jnp.float32)
        last = [[zero] * tiles, [zero] * tiles]
        for g in range(n // 8 + 1):
            r = 8 * g
            if g < n // 8:
                o_re, o_im = [
                    jnp.concatenate([win[part, j, r : r + 8, :] for j in range(tiles)], 1) for part in range(2)
                ]
                t_re = t_im = None
                for m in range(modes):
                    u_re = update[r : r + 8, m * n : (m + 1) * n]
                    u_im = update[n + r : n + r + 8, m * n : (m + 1) * n]
                    p_re = probe[m, 0, r : r + 8, :]
                    p_im = probe[m, 1, r : r + 8, :]
                    a_re = p_re * u_re + p_im * u_im
                    a_im = p_re * u_im - p_im * u_re
                    t_re = a_re if t_re is None else t_re + a_re
                    t_im = a_im if t_im is None else t_im + a_im
                    pgrad[m, 0, r : r + 8, :] += o_re * u_re + o_im * u_im
                    pgrad[m, 1, r : r + 8, :] += o_re * u_im - o_im * u_re
                terms = [
                    [pltpu.roll(t[:, 128 * j : 128 * (j + 1)], low, 0) for j in range(tiles)]
                    for t in (t_re, t_im)
                ]
            else:
                terms = [[zero] * tiles, [zero] * tiles]
            for part in range(2):
                placed = [jnp.where(lower, terms[part][j], last[part][j]) for j in range(tiles)]
                turned = [zero] + [pltpu.roll(v, shift, 1) for v in placed] + [zero]
                for j in range(tiles + 1):
                    block = jnp.where(fresh, turned[j + 1], turned[j])
                    grad[part, pl.ds(floor + r, 8), pl.ds(base + 128 * j, 128)] += block
            last = terms

    height, width = grad.shape[1] - NOTE_ROWS, grad.shape[2]
    strips = [(part, r, c) for part in range(2) for c in (0, width - 128) for r in range(0, height, 8)]
    peak = jnp.zeros((8, 128), jnp.float32)
    for part, r, c in strips:
        peak = jnp.maximum(peak, jnp.abs(grad[part, r : r + 8, c : c + 128]))
    power = jnp.ceil(jnp.log2(jnp.full((8, 128), jnp.maximum(jnp.max(peak), 1e-30))))
    factor = jnp.exp2(HEADROOM - power)
    for part, r, c in strips:
        grad[part, r : r + 8, c : c + 128] *= factor
    for part in range(2):
        for c in (0, width - 128):
            for r in range(height, height + NOTE_ROWS, 8):
                grad[part, r : r + 8, c : c + 128] = power


ANYWHERE = pl.BlockSpec(memory_space=pl.ANY)
SCALARS = pl.BlockSpec(memory_space=pltpu.SMEM)
LOCAL = pl.BlockSpec(memory_space=pltpu.VMEM)


def call(kernel, name, ins, outs, in_specs, out_specs, scratch, vmem):
    return pl.pallas_call(
        kernel,
        in_specs=in_specs,
        out_specs=out_specs,
        scratch_shapes=scratch,
        out_shape=outs,
        compiler_params=pltpu.CompilerParams(vmem_limit_bytes=vmem),
        name=name,
    )(*ins)


def exit_waves(slots, count, tops, lefts, probe, pieces, half, tile):
    modes, _, n, _ = probe.shape
    parts = parts_of(half, tile)
    wide = tile + 2 * half
    line = jnp.arange(n, dtype=jnp.int32)
    below = jnp.concatenate([line[0 : n // 2 : 2], line[1 : n // 2 : 2]])
    even = dft_table(below, line[0::2], n, 1)
    odd = dft_table(below, line[1::2], n, 1)
    probe = probe.reshape(modes, 2, n // 2, 2, n).swapaxes(2, 3)
    outs = (
        pltpu.HBM((slots, modes * n, 2 * n), jnp.bfloat16),
        pltpu.HBM((slots, 2, n // 128, n, 128), jnp.float32),
    )
    return call(
        functools.partial(waves_kernel, points=n, modes=modes, parts=parts),
        "waves",
        (count, tops, lefts, probe, even, odd, *pieces),
        outs,
        [SCALARS] * 3 + [ANYWHERE] * (3 + len(parts)),
        [pl.BlockSpec(memory_space=pltpu.HBM)] * 2,
        [pltpu.VMEM(a.shape, a.dtype) for a in (probe, even, odd)]
        + [
            pltpu.VMEM((2, wide, wide), jnp.float32),
            pltpu.VMEM((2, n, modes * n), jnp.bfloat16),
            pltpu.VMEM((2,) + outs[0].shape[1:], outs[0].dtype),
            pltpu.VMEM((2,) + outs[1].shape[1:], outs[1].dtype),
            pltpu.SemaphoreType.DMA((sum(map(len, parts)) + 3,)),
            pltpu.SemaphoreType.DMA((2, 2)),
        ],
        VMEM_BYTES,
    )


def gradients(order, count, tops, lefts, raw, half_done, win, probe, resample, half, tile):
    modes, _, n, _ = probe.shape
    wide = tile + 2 * half
    line = jnp.arange(n, dtype=jnp.int32)
    low = line[: n // 2]
    sides = [line[0::2], line[1::2]]
    turn = jnp.concatenate([dft_table(line, q, n, -1) for q in sides], 1)
    row_even, row_odd = [dft_table(q, low, n, 1) for q in sides]
    col_even, col_odd = [dft_table(low, q, n, -1) for q in sides]
    res = resample.reshape(2, n // 4, 2, n).swapaxes(1, 2).reshape(n, n)
    res_t = resample.reshape(n // 2, 2, n).swapaxes(0, 1).reshape(n, n).T
    outs = [pltpu.VMEM(probe.shape, jnp.float32), pltpu.VMEM((2, wide + NOTE_ROWS, wide), jnp.float32)]
    constant = (probe, turn, row_even, row_odd, col_even, col_odd, res, res_t)
    return call(
        functools.partial(frames_kernel, points=n, modes=modes),
        "frames",
        (order, count, tops, lefts, raw, half_done, win, *constant),
        outs,
        [SCALARS] * 4 + [ANYWHERE] * (3 + len(constant)),
        [LOCAL] * 2,
        [pltpu.VMEM(a.shape, a.dtype) for a in constant]
        + [
            pltpu.VMEM((2, n, n), raw.dtype),
            pltpu.VMEM((2,) + half_done.shape[1:], half_done.dtype),
            pltpu.VMEM((2,) + win.shape[1:], win.dtype),
            pltpu.VMEM((modes * n, 2 * n), jnp.float32),
            pltpu.VMEM((modes * n, 2 * n), jnp.bfloat16),
            pltpu.VMEM((2, n, modes * n), jnp.bfloat16),
            pltpu.VMEM((2 * n, modes * n), jnp.float32),
            pltpu.VMEM((n, n), jnp.float32),
            pltpu.SemaphoreType.DMA((2, 3)),
            pltpu.SemaphoreType.DMA((len(constant),)),
        ],
        VMEM_BYTES,
    )


def to_neighbour(value, axes, step):
    size = lax.axis_size(axes)
    pairs = [(i, i + step) for i in range(size) if 0 <= i + step < size]
    return lax.ppermute(value, axes, pairs)


def merge_kernel(grad, above, below, left, right, out, sem, *, half, tile):
    end = half + tile
    copy = pltpu.make_async_copy(grad.at[:, pl.ds(half, tile), pl.ds(half, tile)], out, sem)
    copy.start()
    copy.wait()
    for part in range(2):
        out[part, :half, :] += above[part]
        out[part, tile - half :, :] += below[part]
        out[part, :, :half] += left[part, half:end, :]
        out[part, :, tile - half :] += right[part, half:end, :]


def merge(grad, pieces, half, tile):
    return call(
        functools.partial(merge_kernel, half=half, tile=tile),
        "merge",
        (grad, *pieces),
        jax.ShapeDtypeStruct((2, tile, tile), jnp.float32),
        [ANYWHERE] + [LOCAL] * 4,
        LOCAL,
        [pltpu.SemaphoreType.DMA],
        16 * 2**20,
    )


def peers(values, axes):
    size = lax.axis_size(axes)
    return [lax.ppermute(v, axes, [(i, i ^ (k + 1)) for i in range(size)]) for k, v in enumerate(values)]


def scattered(value, axes):
    size, place = lax.axis_size(axes), lax.axis_index(axes)
    length = value.shape[0] // size
    parts = [lax.dynamic_slice_in_dim(value, (place ^ k) * length, length, 0) for k in range(size)]
    return sum(peers(parts[1:], axes), parts[0])


def gathered(value, axes):
    size, place = lax.axis_size(axes), lax.axis_index(axes)
    held = [value] + peers([value] * (size - 1), axes)
    parts = []
    for j in range(size):
        part = held[size - 1]
        for k in range(size - 1):
            part = jnp.where(place == j ^ k, held[k], part)
        parts.append(part)
    return jnp.concatenate(parts, 0)


def summed(value, axes):
    held = [value] + peers([value] * (lax.axis_size(axes) - 1), axes)
    while len(held) > 1:
        held = [a + b for a, b in zip(held[::2], held[1::2])]
    return held[0]


def shards(object_field, probe, raw_counts, resample_delta, tile_row, offsets):
    modes, _, points, _ = probe.shape
    half = points // 2
    tile = object_field.shape[1]
    tile_rows = lax.axis_size(ROW)
    frame_total = raw_counts.shape[0] * tile_rows * lax.axis_size(COL)
    above = to_neighbour(object_field[:, tile - half :, :], ROW, 1)
    below = to_neighbour(object_field[:, :half, :], ROW, -1)
    left = to_neighbour(object_field[:, :, tile - half :], COL, 1)
    right = to_neighbour(object_field[:, :, :half], COL, -1)
    corners = [
        jnp.concatenate([a[:, :, cols] for a in (above, below)], 1)
        for cols in (slice(tile - half, None), slice(0, half))
    ]
    corners = [to_neighbour(a, COL, step) for a, step in zip(corners, (1, -1))]
    target = tile_row[:, 0]
    raw_counts, corners = lax.optimization_barrier((raw_counts, corners))
    slots = spread(target, raw_counts, tile_rows)
    arrived = lax.all_to_all(slots, ROW, split_axis=0, concat_axis=0, tiled=True)
    slot_ids = jnp.arange(tile_rows, dtype=jnp.int32)
    picks = (target[:, None] == slot_ids[None, :]).astype(jnp.int32)
    requests = jnp.stack(
        [jnp.sum(picks * offsets[:, 0:1], 0), jnp.sum(picks * offsets[:, 1:2], 0), jnp.sum(picks, 0)], 1
    )
    received = lax.all_to_all(requests, ROW, split_axis=0, concat_axis=0, tiled=True)
    live = received[:, 2]
    count = jnp.sum(live)
    rank = jnp.sum(jnp.where(slot_ids[None, :] < slot_ids[:, None], live[None, :], 0), 1)
    place = jnp.minimum(slot_ids, jnp.maximum(count - 1, 0))
    hit = (rank[None, :] == place[:, None]) & (live[None, :] > 0)
    order = jnp.sum(jnp.where(hit, slot_ids[None, :], 0), 1)
    tops = jnp.sum(jnp.where(hit, received[None, :, 0], 0), 1)
    lefts = jnp.sum(jnp.where(hit, received[None, :, 1], 0), 1)
    count = count[None]
    resample = (jnp.eye(points, dtype=jnp.float32) + resample_delta).astype(jnp.bfloat16)
    pieces = [object_field, above, below, left, right, *corners]
    half_done, win = exit_waves(tile_rows, count, tops, lefts, probe, pieces, half, tile)
    probe_total, grad = gradients(
        order, count, tops, lefts, arrived, half_done, win, probe, resample, half, tile
    )
    total = scattered(probe_total.reshape(-1, points), "core")
    from_west = to_neighbour(grad[:, :, half + tile :].astype(jnp.float16), COL, 1)
    from_east = to_neighbour(grad[:, :, :half].astype(jnp.float16), COL, -1)
    total = scattered(scattered(total, "x"), "z")
    total = summed(total, ("y_far", "y_near")) * (1.0 / math.sqrt(frame_total))
    total, from_west, from_east = lax.optimization_barrier((total, from_west, from_east))
    from_west, from_east = [
        strip[:, :-NOTE_ROWS, :].astype(jnp.float32) * jnp.exp2(strip[0, -1, 0].astype(jnp.float32) - HEADROOM)
        for strip in (from_west, from_east)
    ]

    def with_corners(rows):
        strip = grad[:, rows, half : half + tile]
        strip = strip.at[:, :, :half].add(from_west[:, rows, :])
        return strip.at[:, :, tile - half :].add(from_east[:, rows, :])

    from_below = to_neighbour(with_corners(slice(0, half)), ROW, -1)
    from_above = to_neighbour(with_corners(slice(half + tile, 2 * half + tile)), ROW, 1)
    total = gathered(gathered(total, "z"), "x")
    total, from_above, from_below = lax.optimization_barrier((total, from_above, from_below))
    total = gathered(total, "core")
    object_grad = merge(grad, [from_above, from_below, from_west, from_east], half, tile)
    return (object_grad, total.reshape(probe.shape))


def solution(mesh):
    torus = Mesh(mesh.devices.reshape(4, 2, 2, 4, 2), ROW_COL)
    return jax.shard_map(
        shards,
        mesh=torus,
        in_specs=(
            P(None, ROW, COL),
            P(),
            P(ROW_COL, None, None),
            P(),
            P(ROW_COL, None),
            P(ROW_COL, None),
        ),
        out_specs=(P(None, ROW, COL), P()),
        check_vma=False,
    )
```

time: 299 us -> 223 us (0.75)
  waiting for transfers between devices: 102 us -> 43.3 us
  Pallas kernels: 58.1 us -> 29.8 us
  local copies, waits for them, and re-layouts: 8.7 us -> 17 us
  other arithmetic: 8.38 us -> 14.7 us
  starting transfers between devices: 119 us -> 115 us
    ppermute x26 -> x27, waiting for transfers between devices: 102 us -> 43.3 us  [the longest x10 27.3 us: to_neighbour(): return lax.ppermute(value, axes, pairs)]
    pallas_call x1, Pallas kernels: 25.6 us -> 2.63 us  [spread(): pl.pallas_call(spread_kernel, grid_spec=pltpu.PrefetchScalarGridSpec(num_...]
    ppermute x26 -> x27, starting transfers between devices: 105 us -> 98 us  [the longest x17 57.9 us: peers(): lax.ppermute(v, axes, [(i, i ^ k + 1) for i in range(size)])]
    pallas_call x2 -> x3, Pallas kernels: 32.5 us -> 27.2 us  [call(): pl.pallas_call(kernel, in_specs=in_specs, out_specs=out_specs, scratch_sh...]
    unnamed x41 -> x24, local copies, waits for them, and re-layouts: 1.95 us -> 6.46 us
    slice x3 -> x13, local copies, waits for them, and re-layouts: 3.1 us -> 7.28 us  [the longest x2 1.43 us: exit_waves(): below = jnp.concatenate([line[0:n // 2:2], line[1:n // 2:2]])]
    all_to_all x1, starting transfers between devices: 5.45 us -> 9.47 us  [shards(): lax.all_to_all(slots, ROW, split_axis=0, concat_axis=0, tiled=True)]
    another operation x2 -> x3, other arithmetic: 2.1 us -> 5.48 us
  transfers between devices with their start and end apart: 28 -> 29, of which waited for: 15 -> 10; matrix products, arithmetic and copies ran while one was open for 3% -> 10% of each run, Pallas kernels for 10% -> 6%
where the time goes in v3:
time: 223 us
  starting transfers between devices  115 us (52%)
  waiting for transfers between devices  43.3 us (19%)
  Pallas kernels  29.8 us (13%)
  local copies, waits for them, and re-layouts  17 us (8%)
  other arithmetic  14.7 us (7%)
  between operations  3.22 us (1%)
    ppermute x17, starting transfers between devices, peers(): lax.ppermute(v, axes, [(i, i ^ k + 1) for i in range(size)])  57.9 us
    ppermute x10, starting transfers between devices, to_neighbour(): return lax.ppermute(value, axes, pairs)  40.1 us
    ppermute x10, waiting for transfers between devices, to_neighbour(): return lax.ppermute(value, axes, pairs)  27.3 us
    pallas_call x3, Pallas kernels, call(): pl.pallas_call(kernel, in_specs=in_specs, out_specs=out_specs, scratch_sh...  27.2 us
    ppermute x17, waiting for transfers between devices, peers(): lax.ppermute(v, axes, [(i, i ^ k + 1) for i in range(size)])  16 us
    all_to_all x1, starting transfers between devices, shards(): lax.all_to_all(slots, ROW, split_axis=0, concat_axis=0, tiled=True)  9.47 us
    all_to_all x1, starting transfers between devices, shards(): lax.all_to_all(requests, ROW, split_axis=0, concat_axis=0, tiled=True)  7.38 us
    unnamed x24, local copies, waits for them, and re-layouts  6.46 us
  transfers between devices with their start and end apart: 29, of which 10 were waited for; matrix products, arithmetic and copies ran while one was open for 10% of the time, Pallas kernels for 6%

profile of v3, /device:TPU:1, one launch (start us, length us, event | category | flops | bytes accessed | tf_op | source)
XLA Modules:
  0.0 222.9 jit_solution(1110079079630774030)
XLA Ops:
  2.0 6.2 %collective-permute-start = (f32[2,128,512]{2,1,0:T(8,128)S(1)}, f32[2,128,512]{2,1,0:T(8,128)S(1)}, u32[]{:S(2)}, u32[]{:S(2)}) collective-permute-start(f32[2,128,512]{2,1,0:T(8,128)S(1)} %get-tuple-element.90), channel_id=1, source_target_pairs={{0,8},{8,16},{16,24},{24,32},{32,40},{40,48},{48,56},{56,64},{64,7... | collective-permute-start | bytes 1572872 | tf_op jit(solution)/shard_map/ppermute | solution.py:403
  10.9 7.4 %all-to-all-start = ((s32[16,1,3]{2,1,0:T(1,128)}), s32[16,1,3]{2,1,0:T(1,128)S(1)}, u32[]{:S(2)}, u32[]{:S(2)}) async-start(s32[16,1,3]{2,1,0:T(1,128)} %copy.20), calls=%async_computation | async-start | bytes 16384 | tf_op jit(solution)/shard_map/all_to_all | solution.py:486
  21.6 4.0 %collective-permute-start.2 = (f32[2,256,128]{2,1,0:T(8,128)S(1)}, f32[2,256,128]{2,1,0:T(8,128)S(1)}, u32[]{:S(2)}, u32[]{:S(2)}) collective-permute-start(f32[2,256,128]{2,1,0:T(8,128)S(1)} %pad_maximum_fusion.2), channel_id=1, source_target_pairs={{0,1},{1,2},{2,3},{3,4},{4,5},{5,6},{6,7},{8,9},{9,10},{10,11},{11... | collective-permute-start | bytes 786440 | tf_op jit(solution)/shard_map/ppermute | solution.py:403
  26.7 4.1 %collective-permute-start.4 = (f32[2,512,128]{2,1,0:T(8,128)}, f32[2,512,128]{2,1,0:T(8,128)}, u32[]{:S(2)}, u32[]{:S(2)}) collective-permute-start(f32[2,512,128]{2,1,0:T(8,128)} %get-tuple-element.89), channel_id=1, source_target_pairs={{0,1},{1,2},{2,3},{3,4},{4,5},{5,6},{6,7},{8,9},{9,10},{10,11},{11... | collective-permute-start | bytes 1572872 | tf_op jit(solution)/shard_map/ppermute | solution.py:403
  32.0 2.6 %spread.1 = bf16[16,256,256]{2,1,0:T(8,128)(2,1)} custom-call(s32[6]{0:T(128)} %bitcast.51, bf16[6,256,256]{2,1,0:T(8,128)(2,1)} %counts), custom_call_target="tpu_custom_call" | custom-call | tf_op jit(solution)/shard_map/spread/pallas_call | solution.py:46
  34.7 9.5 %all-to-all-start.1 = ((bf16[16,256,256]{2,1,0:T(8,128)(2,1)}), bf16[16,256,256]{2,1,0:T(8,128)(2,1)}, u32[]{:S(2)}, u32[]{:S(2)}) async-start(bf16[16,256,256]{2,1,0:T(8,128)(2,1)} %spread.1), calls=%async_computation.1 | async-start | bytes 4194304 | tf_op jit(solution)/shard_map/all_to_all | solution.py:480
  59.4 15.9 %collective-permute-done.5.refs_4_ = f32[2,512,128]{2,1,0:T(8,128)} collective-permute-done((f32[2,512,128]{2,1,0:T(8,128)}, f32[2,512,128]{2,1,0:T(8,128)}, u32[]{:S(2)}, u32[]{:S(2)}) %collective-permute-start.5) | collective-permute-done | bytes 524320 | tf_op jit(solution)/shard_map/ppermute | solution.py:403
  75.2 9.1 %waves.1 = (bf16[16,768,512]{2,1,0:T(8,128)(2,1)}, f32[16,2,2,256,128]{4,3,2,1,0:T(8,128)}) custom-call(s32[1]{0:T(128)} %bitcast.9.count, s32[16]{0:T(128)S(1)} %get-tuple-element.77.tops, s32[16]{0:T(128)S(1)} %get-tuple-element.76.lefts, f32[3,2,2,128,256]{4,3,2,1,0:T(8,128)} %bitcast.44, bf16[256,256]{1,0:T(8,128)(2,1)S(1)} %get-tuple-element.155.even_all, ...), custom_call_target="tpu_custom_call" | custom-call | tf_op jit(solution)/shard_map/waves/pallas_call | solution.py:319
  84.4 16.2 %frames.1 = (f32[3,2,256,256]{3,2,1,0:T(8,128)S(1)}, f32[2,784,768]{2,1,0:T(8,128)S(1)}) custom-call(s32[16]{0:T(128)} %get-tuple-element.78.order, s32[1]{0:T(128)} %bitcast.9.count, s32[16]{0:T(128)} %copy-done.3, s32[16]{0:T(128)} %copy-done.2, bf16[16,256,256]{2,1,0:T(8,128)(2,1)} %all-to-all-done.1.raw_all, ...), custom_call_target="tpu_custom_call" | custom-call | tf_op jit(solution)/shard_map/frames/pallas_call | solution.py:319
  102.9 2.2 %collective-permute-done.6 = f32[768,256]{1,0:T(8,128)S(1)} collective-permute-done((f32[768,256]{1,0:T(8,128)S(1)}, f32[768,256]{1,0:T(8,128)S(1)}, u32[]{:S(2)}, u32[]{:S(2)}) %collective-permute-start.6) | collective-permute-done | bytes 786464 | tf_op jit(solution)/shard_map/ppermute | solution.py:433
  105.3 2.5 %collective-permute-start.7 = (f32[192,256]{1,0:T(8,128)S(1)}, f32[192,256]{1,0:T(8,128)S(1)}, u32[]{:S(2)}, u32[]{:S(2)}) collective-permute-start(f32[192,256]{1,0:T(8,128)S(1)} %get-tuple-element.99), channel_id=1, source_target_pairs={{0,32},{32,0},{64,96},{96,64},{1,33},{33,1},{65,97},{97,65},{2,34}... | collective-permute-start | bytes 589832 | tf_op jit(solution)/shard_map/ppermute | solution.py:433
  107.8 2.3 %collective-permute-start.8 = (f32[192,256]{1,0:T(8,128)S(1)}, f32[192,256]{1,0:T(8,128)S(1)}, u32[]{:S(2)}, u32[]{:S(2)}) collective-permute-start(f32[192,256]{1,0:T(8,128)S(1)} %get-tuple-element.101), channel_id=1, source_target_pairs={{0,64},{32,96},{64,0},{96,32},{1,65},{33,97},{65,1},{97,33},{2,66}... | collective-permute-start | bytes 589832 | tf_op jit(solution)/shard_map/ppermute | solution.py:433
  110.3 2.7 %convert.136 = f16[2,784,768]{2,1,0:T(8,128)(2,1)S(1)} convert(f32[2,784,768]{2,1,0:T(8,128)} %copy-done) | non-fusion elementwise | flops 1204224 | bytes 7225344 | tf_op jit(solution)/shard_map/convert.1
  113.0 6.3 %collective-permute-done.8 = f32[192,256]{1,0:T(8,128)S(1)} collective-permute-done((f32[192,256]{1,0:T(8,128)S(1)}, f32[192,256]{1,0:T(8,128)S(1)}, u32[]{:S(2)}, u32[]{:S(2)}) %collective-permute-start.8) | collective-permute-done | bytes 196640 | tf_op jit(solution)/shard_map/ppermute | solution.py:433
  121.5 4.4 %collective-permute-start.10 = (f32[48,256]{1,0:T(8,128)S(1)}, f32[48,256]{1,0:T(8,128)S(1)}, u32[]{:S(2)}, u32[]{:S(2)}) collective-permute-start(f32[48,256]{1,0:T(8,128)S(1)} %get-tuple-element.110), channel_id=1, source_target_pairs={{0,2},{2,0},{4,6},{6,4},{1,3},{3,1},{5,7},{7,5},{8,10},{10,8},{12,... | collective-permute-start | bytes 147464 | tf_op jit(solution)/shard_map/ppermute | solution.py:433
  125.8 5.5 %collective-permute-start.11 = (f32[48,256]{1,0:T(8,128)S(1)}, f32[48,256]{1,0:T(8,128)S(1)}, u32[]{:S(2)}, u32[]{:S(2)}) collective-permute-start(f32[48,256]{1,0:T(8,128)S(1)} %get-tuple-element.112), channel_id=1, source_target_pairs={{0,4},{2,6},{4,0},{6,2},{1,5},{3,7},{5,1},{7,3},{8,12},{10,14},{12... | collective-permute-start | bytes 147464 | tf_op jit(solution)/shard_map/ppermute | solution.py:433
  131.7 11.6 %collective-permute-start.16 = (f16[2,784,128]{2,1,0:T(8,128)(2,1)S(1)}, f16[2,784,128]{2,1,0:T(8,128)(2,1)S(1)}, u32[]{:S(2)}, u32[]{:S(2)}) collective-permute-start(f16[2,784,128]{2,1,0:T(8,128)(2,1)S(1)} %get-tuple-element.87), channel_id=1, source_target_pairs={{0,1},{1,2},{2,3},{3,4},{4,5},{5,6},{6,7},{8,9},{9,10},{10,11},{11... | collective-permute-start | bytes 1204232 | tf_op jit(solution)/shard_map/ppermute | solution.py:403
  146.8 25.8 %collective-permute-start.14 = (f32[48,256]{1,0:T(8,128)S(1)}, f32[48,256]{1,0:T(8,128)S(1)}, u32[]{:S(2)}, u32[]{:S(2)}) collective-permute-start(f32[48,256]{1,0:T(8,128)S(1)} %add_add_fusion.1), channel_id=1, source_target_pairs={{0,16},{1,17},{16,0},{17,1},{2,18},{3,19},{18,2},{19,3},{4,20},{5,... | collective-permute-start | bytes 147464 | tf_op jit(solution)/shard_map/ppermute | solution.py:433
  173.9 4.3 %collective-permute-done.14 = f32[48,256]{1,0:T(8,128)S(1)} collective-permute-done((f32[48,256]{1,0:T(8,128)S(1)}, f32[48,256]{1,0:T(8,128)S(1)}, u32[]{:S(2)}, u32[]{:S(2)}) %collective-permute-start.14) | collective-permute-done | bytes 49184 | tf_op jit(solution)/shard_map/ppermute | solution.py:433
  178.2 10.5 %collective-permute-start.18 = (f32[48,256]{1,0:T(8,128)S(1)}, f32[48,256]{1,0:T(8,128)S(1)}, u32[]{:S(2)}, u32[]{:S(2)}) collective-permute-start(f32[48,256]{1,0:T(8,128)S(1)} %add_multiply_fusion), channel_id=1, source_target_pairs={{0,4},{2,6},{4,0},{6,2},{1,5},{3,7},{5,1},{7,3},{8,12},{10,14},{12... | collective-permute-start | bytes 147464 | tf_op jit(solution)/shard_map/ppermute | solution.py:433
  197.8 6.3 %collective-permute-start.24 = (f32[2,128,512]{2,1,0:T(8,128)S(1)}, f32[2,128,512]{2,1,0:T(8,128)S(1)}, u32[]{:S(2)}, u32[]{:S(2)}) collective-permute-start(f32[2,128,512]{2,1,0:T(8,128)S(1)} %get-tuple-element.95), channel_id=1, source_target_pairs={{0,8},{8,16},{16,24},{24,32},{32,40},{40,48},{48,56},{56,64},{64,7... | collective-permute-start | bytes 1572872 | tf_op jit(solution)/shard_map/ppermute | solution.py:403
  206.5 3.7 %collective-permute-done.24.above = f32[2,128,512]{2,1,0:T(8,128)S(1)} collective-permute-done((f32[2,128,512]{2,1,0:T(8,128)S(1)}, f32[2,128,512]{2,1,0:T(8,128)S(1)}, u32[]{:S(2)}, u32[]{:S(2)}) %collective-permute-start.24) | collective-permute-done | bytes 524320 | tf_op jit(solution)/shard_map/ppermute | solution.py:403
  210.2 5.9 %collective-permute-done.25.below = f32[2,128,512]{2,1,0:T(8,128)S(1)} collective-permute-done((f32[2,128,512]{2,1,0:T(8,128)S(1)}, f32[2,128,512]{2,1,0:T(8,128)S(1)}, u32[]{:S(2)}, u32[]{:S(2)}) %collective-permute-start.25) | collective-permute-done | bytes 524320 | tf_op jit(solution)/shard_map/ppermute | solution.py:403
  216.1 2.4 %copy-done.1 = f32[2,784,768]{2,1,0:T(8,128)S(1)} copy-done((f32[2,784,768]{2,1,0:T(8,128)S(1)}, f32[2,784,768]{2,1,0:T(8,128)}, u32[]{:S(2)}) %copy-start.1) | copy-done | bytes 4816920
  (124 shorter events, 48.4 us)
Async XLA Ops:
  2.0 18.0 %collective-permute-start = (f32[2,128,512]{2,1,0:T(8,128)S(1)}, f32[2,128,512]{2,1,0:T(8,128)S(1)}, u32[]{:S(2)}, u32[]{:S(2)}) collective-permute-start(f32[2,128,512]{2,1,0:T(8,128)S(1)} %get-tuple-element.90), channel_id=1, source_target_pairs={{0,8},{8,16},{16,24},{24,32},{32,40},{40,48},{48,56},{56,64},{64,7... | collective-permute-start | bytes 1572872 | tf_op jit(solution)/shard_map/ppermute | solution.py:403
  8.2 12.0 %collective-permute-start.1 = (f32[2,128,512]{2,1,0:T(8,128)S(1)}, f32[2,128,512]{2,1,0:T(8,128)S(1)}, u32[]{:S(2)}, u32[]{:S(2)}) collective-permute-start(f32[2,128,512]{2,1,0:T(8,128)S(1)} %get-tuple-element.91), channel_id=1, source_target_pairs={{8,0},{16,8},{24,16},{32,24},{40,32},{48,40},{56,48},{64,56},{72,6... | collective-permute-start | bytes 1572872 | tf_op jit(solution)/shard_map/ppermute | solution.py:403
  10.9 23.7 %all-to-all-start = ((s32[16,1,3]{2,1,0:T(1,128)}), s32[16,1,3]{2,1,0:T(1,128)S(1)}, u32[]{:S(2)}, u32[]{:S(2)}) async-start(s32[16,1,3]{2,1,0:T(1,128)} %copy.20), calls=%async_computation | async-start | bytes 16384 | tf_op jit(solution)/shard_map/all_to_all | solution.py:486
  20.2 11.8 %collective-permute-start.3 = (f32[2,256,128]{2,1,0:T(8,128)S(1)}, f32[2,256,128]{2,1,0:T(8,128)S(1)}, u32[]{:S(2)}, u32[]{:S(2)}) collective-permute-start(f32[2,256,128]{2,1,0:T(8,128)S(1)} %pad_maximum_fusion.3), channel_id=1, source_target_pairs={{1,0},{2,1},{3,2},{4,3},{5,4},{6,5},{7,6},{9,8},{10,9},{11,10},{12... | collective-permute-start | bytes 786440 | tf_op jit(solution)/shard_map/ppermute | solution.py:403
  21.6 10.4 %collective-permute-start.2 = (f32[2,256,128]{2,1,0:T(8,128)S(1)}, f32[2,256,128]{2,1,0:T(8,128)S(1)}, u32[]{:S(2)}, u32[]{:S(2)}) collective-permute-start(f32[2,256,128]{2,1,0:T(8,128)S(1)} %pad_maximum_fusion.2), channel_id=1, source_target_pairs={{0,1},{1,2},{2,3},{3,4},{4,5},{5,6},{6,7},{8,9},{9,10},{10,11},{11... | collective-permute-start | bytes 786440 | tf_op jit(solution)/shard_map/ppermute | solution.py:403
  26.7 32.7 %collective-permute-start.4 = (f32[2,512,128]{2,1,0:T(8,128)}, f32[2,512,128]{2,1,0:T(8,128)}, u32[]{:S(2)}, u32[]{:S(2)}) collective-permute-start(f32[2,512,128]{2,1,0:T(8,128)} %get-tuple-element.89), channel_id=1, source_target_pairs={{0,1},{1,2},{2,3},{3,4},{4,5},{5,6},{6,7},{8,9},{9,10},{10,11},{11... | collective-permute-start | bytes 1572872 | tf_op jit(solution)/shard_map/ppermute | solution.py:403
  30.7 44.5 %collective-permute-start.5 = (f32[2,512,128]{2,1,0:T(8,128)}, f32[2,512,128]{2,1,0:T(8,128)}, u32[]{:S(2)}, u32[]{:S(2)}) collective-permute-start(f32[2,512,128]{2,1,0:T(8,128)} %get-tuple-element.88), channel_id=1, source_target_pairs={{1,0},{2,1},{3,2},{4,3},{5,4},{6,5},{7,6},{9,8},{10,9},{11,10},{12... | collective-permute-start | bytes 1572872 | tf_op jit(solution)/shard_map/ppermute | solution.py:403
  34.7 49.7 %all-to-all-start.1 = ((bf16[16,256,256]{2,1,0:T(8,128)(2,1)}), bf16[16,256,256]{2,1,0:T(8,128)(2,1)}, u32[]{:S(2)}, u32[]{:S(2)}) async-start(bf16[16,256,256]{2,1,0:T(8,128)(2,1)} %spread.1), calls=%async_computation.1 | async-start | bytes 4194304 | tf_op jit(solution)/shard_map/all_to_all | solution.py:480
  105.3 7.6 %collective-permute-start.7 = (f32[192,256]{1,0:T(8,128)S(1)}, f32[192,256]{1,0:T(8,128)S(1)}, u32[]{:S(2)}, u32[]{:S(2)}) collective-permute-start(f32[192,256]{1,0:T(8,128)S(1)} %get-tuple-element.99), channel_id=1, source_target_pairs={{0,32},{32,0},{64,96},{96,64},{1,33},{33,1},{65,97},{97,65},{2,34}... | collective-permute-start | bytes 589832 | tf_op jit(solution)/shard_map/ppermute | solution.py:433
  107.8 11.5 %collective-permute-start.8 = (f32[192,256]{1,0:T(8,128)S(1)}, f32[192,256]{1,0:T(8,128)S(1)}, u32[]{:S(2)}, u32[]{:S(2)}) collective-permute-start(f32[192,256]{1,0:T(8,128)S(1)} %get-tuple-element.101), channel_id=1, source_target_pairs={{0,64},{32,96},{64,0},{96,32},{1,65},{33,97},{65,1},{97,33},{2,66}... | collective-permute-start | bytes 589832 | tf_op jit(solution)/shard_map/ppermute | solution.py:433
  110.1 11.2 %collective-permute-start.9 = (f32[192,256]{1,0:T(8,128)S(1)}, f32[192,256]{1,0:T(8,128)S(1)}, u32[]{:S(2)}, u32[]{:S(2)}) collective-permute-start(f32[192,256]{1,0:T(8,128)S(1)} %get-tuple-element.100), channel_id=1, source_target_pairs={{0,96},{32,64},{64,32},{96,0},{1,97},{33,65},{65,33},{97,1},{2,98}... | collective-permute-start | bytes 589832 | tf_op jit(solution)/shard_map/ppermute | solution.py:433
  121.5 23.1 %collective-permute-start.10 = (f32[48,256]{1,0:T(8,128)S(1)}, f32[48,256]{1,0:T(8,128)S(1)}, u32[]{:S(2)}, u32[]{:S(2)}) collective-permute-start(f32[48,256]{1,0:T(8,128)S(1)} %get-tuple-element.110), channel_id=1, source_target_pairs={{0,2},{2,0},{4,6},{6,4},{1,3},{3,1},{5,7},{7,5},{8,10},{10,8},{12,... | collective-permute-start | bytes 147464 | tf_op jit(solution)/shard_map/ppermute | solution.py:433
  125.8 18.7 %collective-permute-start.11 = (f32[48,256]{1,0:T(8,128)S(1)}, f32[48,256]{1,0:T(8,128)S(1)}, u32[]{:S(2)}, u32[]{:S(2)}) collective-permute-start(f32[48,256]{1,0:T(8,128)S(1)} %get-tuple-element.112), channel_id=1, source_target_pairs={{0,4},{2,6},{4,0},{6,2},{1,5},{3,7},{5,1},{7,3},{8,12},{10,14},{12... | collective-permute-start | bytes 147464 | tf_op jit(solution)/shard_map/ppermute | solution.py:433
  131.3 13.3 %collective-permute-start.12 = (f32[48,256]{1,0:T(8,128)S(1)}, f32[48,256]{1,0:T(8,128)S(1)}, u32[]{:S(2)}, u32[]{:S(2)}) collective-permute-start(f32[48,256]{1,0:T(8,128)S(1)} %get-tuple-element.111), channel_id=1, source_target_pairs={{0,6},{2,4},{4,2},{6,0},{1,7},{3,5},{5,3},{7,1},{8,14},{10,12},{12... | collective-permute-start | bytes 147464 | tf_op jit(solution)/shard_map/ppermute | solution.py:433
  131.7 46.5 %collective-permute-start.16 = (f16[2,784,128]{2,1,0:T(8,128)(2,1)S(1)}, f16[2,784,128]{2,1,0:T(8,128)(2,1)S(1)}, u32[]{:S(2)}, u32[]{:S(2)}) collective-permute-start(f16[2,784,128]{2,1,0:T(8,128)(2,1)S(1)} %get-tuple-element.87), channel_id=1, source_target_pairs={{0,1},{1,2},{2,3},{3,4},{4,5},{5,6},{6,7},{8,9},{9,10},{10,11},{11... | collective-permute-start | bytes 1204232 | tf_op jit(solution)/shard_map/ppermute | solution.py:403
  143.3 34.9 %collective-permute-start.17 = (f16[2,784,128]{2,1,0:T(8,128)(2,1)S(1)}, f16[2,784,128]{2,1,0:T(8,128)(2,1)S(1)}, u32[]{:S(2)}, u32[]{:S(2)}) collective-permute-start(f16[2,784,128]{2,1,0:T(8,128)(2,1)S(1)} %get-tuple-element.86), channel_id=1, source_target_pairs={{1,0},{2,1},{3,2},{4,3},{5,4},{6,5},{7,6},{9,8},{10,9},{11,10},{12... | collective-permute-start | bytes 1204232 | tf_op jit(solution)/shard_map/ppermute | solution.py:403
  144.6 29.3 %collective-permute-start.13 = (f32[48,256]{1,0:T(8,128)S(1)}, f32[48,256]{1,0:T(8,128)S(1)}, u32[]{:S(2)}, u32[]{:S(2)}) collective-permute-start(f32[48,256]{1,0:T(8,128)S(1)} %add_add_fusion.1), channel_id=1, source_target_pairs={{0,1},{1,0},{16,17},{17,16},{2,3},{3,2},{18,19},{19,18},{4,5},{5,4... | collective-permute-start | bytes 147464 | tf_op jit(solution)/shard_map/ppermute | solution.py:433
  146.8 31.4 %collective-permute-start.14 = (f32[48,256]{1,0:T(8,128)S(1)}, f32[48,256]{1,0:T(8,128)S(1)}, u32[]{:S(2)}, u32[]{:S(2)}) collective-permute-start(f32[48,256]{1,0:T(8,128)S(1)} %add_add_fusion.1), channel_id=1, source_target_pairs={{0,16},{1,17},{16,0},{17,1},{2,18},{3,19},{18,2},{19,3},{4,20},{5,... | collective-permute-start | bytes 147464 | tf_op jit(solution)/shard_map/ppermute | solution.py:433
  178.2 15.1 %collective-permute-start.18 = (f32[48,256]{1,0:T(8,128)S(1)}, f32[48,256]{1,0:T(8,128)S(1)}, u32[]{:S(2)}, u32[]{:S(2)}) collective-permute-start(f32[48,256]{1,0:T(8,128)S(1)} %add_multiply_fusion), channel_id=1, source_target_pairs={{0,4},{2,6},{4,0},{6,2},{1,5},{3,7},{5,1},{7,3},{8,12},{10,14},{12... | collective-permute-start | bytes 147464 | tf_op jit(solution)/shard_map/ppermute | solution.py:433
  194.4 11.9 %collective-permute-start.21 = (f32[192,256]{1,0:T(8,128)S(1)}, f32[192,256]{1,0:T(8,128)S(1)}, u32[]{:S(2)}, u32[]{:S(2)}) collective-permute-start(f32[192,256]{1,0:T(8,128)S(1)} %pad_maximum_fusion.4), channel_id=1, source_target_pairs={{0,64},{32,96},{64,0},{96,32},{1,65},{33,97},{65,1},{97,33},{2,66}... | collective-permute-start | bytes 589832 | tf_op jit(solution)/shard_map/ppermute | solution.py:433
  194.9 11.4 %collective-permute-start.22 = (f32[192,256]{1,0:T(8,128)S(1)}, f32[192,256]{1,0:T(8,128)S(1)}, u32[]{:S(2)}, u32[]{:S(2)}) collective-permute-start(f32[192,256]{1,0:T(8,128)S(1)} %pad_maximum_fusion.4), channel_id=1, source_target_pairs={{0,32},{32,0},{64,96},{96,64},{1,33},{33,1},{65,97},{97,65},{2,34}... | collective-permute-start | bytes 589832 | tf_op jit(solution)/shard_map/ppermute | solution.py:433
  196.0 10.3 %collective-permute-start.23 = (f32[192,256]{1,0:T(8,128)S(1)}, f32[192,256]{1,0:T(8,128)S(1)}, u32[]{:S(2)}, u32[]{:S(2)}) collective-permute-start(f32[192,256]{1,0:T(8,128)S(1)} %pad_maximum_fusion.4), channel_id=1, source_target_pairs={{0,96},{32,64},{64,32},{96,0},{1,97},{33,65},{65,33},{97,1},{2,98}... | collective-permute-start | bytes 589832 | tf_op jit(solution)/shard_map/ppermute | solution.py:433
  197.8 12.4 %collective-permute-start.24 = (f32[2,128,512]{2,1,0:T(8,128)S(1)}, f32[2,128,512]{2,1,0:T(8,128)S(1)}, u32[]{:S(2)}, u32[]{:S(2)}) collective-permute-start(f32[2,128,512]{2,1,0:T(8,128)S(1)} %get-tuple-element.95), channel_id=1, source_target_pairs={{0,8},{8,16},{16,24},{24,32},{32,40},{40,48},{48,56},{56,64},{64,7... | collective-permute-start | bytes 1572872 | tf_op jit(solution)/shard_map/ppermute | solution.py:403
  204.1 12.0 %collective-permute-start.25 = (f32[2,128,512]{2,1,0:T(8,128)S(1)}, f32[2,128,512]{2,1,0:T(8,128)S(1)}, u32[]{:S(2)}, u32[]{:S(2)}) collective-permute-start(f32[2,128,512]{2,1,0:T(8,128)S(1)} %get-tuple-element.94), channel_id=1, source_target_pairs={{8,0},{16,8},{24,16},{32,24},{40,32},{48,40},{56,48},{64,56},{72,6... | collective-permute-start | bytes 1572872 | tf_op jit(solution)/shard_map/ppermute | solution.py:403
  (16 other events, 124.1 us)

commit v4 on v3

--- a/solution.py
+++ b/solution.py
@@ -192,7 +192,7 @@
     tiles = n // 128
 
     def arriving(i):
-        slot = lax.rem(i, 2)
+        slot = lax.rem(i, 3)
         return [
             pltpu.make_async_copy(half_all.at[i], half_buffer.at[slot], sems.at[slot, 0]),
             pltpu.make_async_copy(raw_all.at[order[i]], raw_buffer.at[slot], sems.at[slot, 1]),
@@ -216,49 +216,13 @@
     for copy in copies:
         copy.wait()
 
-    @pl.loop(0, count[0])
-    def _(i):
-        for copy in arriving(i):
-            copy.wait()
-        fetch(i + 1)
-        slot = lax.rem(i, 2)
-        half_done, raw, win = half_buffer.at[slot], raw_buffer.at[slot], win_buffer.at[slot]
-        floor, base, low, shift = place_of(tops[i], lefts[i])
-        field[...] = dot(half_done[...], turn[...])
-        first = dot(res[...], raw[...]).astype(jnp.bfloat16)
-        second = dot(first, res_t[...])
-        amp[...] = jnp.sqrt(jnp.maximum(second, 0.0)).astype(jnp.bfloat16).astype(jnp.float32)
-        for r in range(0, n, 16):
-            far = [field[m * n + r : m * n + r + 16, :] for m in range(modes)]
-            total = far[0] * far[0]
-            for m in range(1, modes):
-                total = total + far[m] * far[m]
-            scaling = []
-            for k in range(2):
-                intensity = total[:, 2 * k * mid : (2 * k + 1) * mid] + total[:, (2 * k + 1) * mid : (2 * k + 2) * mid]
-                s = 1.0 - amp[r : r + 16, k * mid : (k + 1) * mid] * lax.rsqrt(jnp.maximum(intensity, 1.0))
-                scaling += [s, s]
-            scaling = jnp.concatenate(scaling, 1)
-            for m in range(modes):
-                rows[m * n + r : m * n + r + 16, :] = (far[m] * scaling).astype(jnp.bfloat16)
-        for m in range(modes):
-            e = dot(rows[m * n : (m + 1) * n, 0:n], row_even[...])
-            o = dot(rows[m * n : (m + 1) * n, n : 2 * n], row_odd[...])
-            for k, both in enumerate(((e + o).astype(jnp.bfloat16), (e - o).astype(jnp.bfloat16))):
-                c = m * n + k * mid
-                for part in range(2):
-                    for block in range(4):
-                        r = part * mid + block // 2 * quarter
-                        stack[block % 2, r : r + quarter, c : c + mid] = both[
-                            block * quarter : (block + 1) * quarter, part * mid : (part + 1) * mid
-                        ]
-        for m in range(modes):
-            c = m * n
-            e = dot(col_even[...], stack[0, :, c : c + n])
-            o = dot(col_odd[...], stack[1, :, c : c + n])
-            for k, both in enumerate((e + o, e - o)):
-                update[k * mid : (k + 1) * mid, c : c + n] = both[:mid]
-                update[n + k * mid : n + (k + 1) * mid, c : c + n] = both[mid:]
+    update[...] = jnp.zeros(update.shape, jnp.float32)
+    win_buffer[2] = jnp.zeros(win_buffer.shape[1:], jnp.float32)
+
+    def collect(i):
+        win = win_buffer.at[lax.rem(i + 3, 3)]
+        at = jnp.maximum(i, 0)
+        floor, base, low, shift = place_of(tops[at], lefts[at])
         fresh = lax.broadcasted_iota(jnp.int32, (8, 128), 1) >= shift
         lower = lax.broadcasted_iota(jnp.int32, (8, 128), 0) >= low
         zero = jnp.zeros((8, 128), jnp.float32)
@@ -295,6 +259,54 @@
                     grad[part, pl.ds(floor + r, 8), pl.ds(base + 128 * j, 128)] += block
             last = terms
 
+    @pl.loop(0, count[0])
+    def _(i):
+        for copy in arriving(i):
+            copy.wait()
+        fetch(i + 1)
+        slot = lax.rem(i, 3)
+        half_done, raw = half_buffer.at[slot], raw_buffer.at[slot]
+        field[...] = dot(half_done[...], turn[...])
+        collect(i - 1)
+        first = dot(res[...], raw[...]).astype(jnp.bfloat16)
+        second = dot(first, res_t[...])
+        amp[...] = jnp.sqrt(jnp.maximum(second, 0.0)).astype(jnp.bfloat16).astype(jnp.float32)
+        for r in range(0, n, 16):
+            far = [field[m * n + r : m * n + r + 16, :] for m in range(modes)]
+            total = far[0] * far[0]
+            for m in range(1, modes):
+                total = total + far[m] * far[m]
+            scaling = []
+            for k in range(2):
+                intensity = total[:, 2 * k * mid : (2 * k + 1) * mid] + total[:, (2 * k + 1) * mid : (2 * k + 2) * mid]
+                s = 1.0 - amp[r : r + 16, k * mid : (k + 1) * mid] * lax.rsqrt(jnp.maximum(intensity, 1.0))
+                scaling += [s, s]
+            scaling = jnp.concatenate(scaling, 1)
+            for m in range(modes):
+                rows[m * n + r : m * n + r + 16, :] = (far[m] * scaling).astype(jnp.bfloat16)
+        for m in range(modes):
+            e = dot(rows[m * n : (m + 1) * n, 0:n], row_even[...])
+            o = dot(rows[m * n : (m + 1) * n, n : 2 * n], row_odd[...])
+            for k, both in enumerate(((e + o).astype(jnp.bfloat16), (e - o).astype(jnp.bfloat16))):
+                c = m * n + k * mid
+                for part in range(2):
+                    for block in range(4):
+                        r = part * mid + block // 2 * quarter
+                        stack[block % 2, r : r + quarter, c : c + mid] = both[
+                            block * quarter : (block + 1) * quarter, part * mid : (part + 1) * mid
+                        ]
+        for m in range(modes):
+            c = m * n
+            e = dot(col_even[...], stack[0, :, c : c + n])
+            o = dot(col_odd[...], stack[1, :, c : c + n])
+            for k, both in enumerate((e + o, e - o)):
+                update[k * mid : (k + 1) * mid, c : c + n] = both[:mid]
+                update[n + k * mid : n + (k + 1) * mid, c : c + n] = both[mid:]
+
+    @pl.when(count[0] > 0)
+    def _():
+        collect(count[0] - 1)
+
     height, width = grad.shape[1] - NOTE_ROWS, grad.shape[2]
     strips = [(part, r, c) for part in range(2) for c in (0, width - 128) for r in range(0, height, 8)]
     peak = jnp.zeros((8, 128), jnp.float32)
@@ -382,15 +394,15 @@
         [LOCAL] * 2,
         [pltpu.VMEM(a.shape, a.dtype) for a in constant]
         + [
-            pltpu.VMEM((2, n, n), raw.dtype),
-            pltpu.VMEM((2,) + half_done.shape[1:], half_done.dtype),
-            pltpu.VMEM((2,) + win.shape[1:], win.dtype),
+            pltpu.VMEM((3, n, n), raw.dtype),
+            pltpu.VMEM((3,) + half_done.shape[1:], half_done.dtype),
+            pltpu.VMEM((3,) + win.shape[1:], win.dtype),
             pltpu.VMEM((modes * n, 2 * n), jnp.float32),
             pltpu.VMEM((modes * n, 2 * n), jnp.bfloat16),
             pltpu.VMEM((2, n, modes * n), jnp.bfloat16),
             pltpu.VMEM((2 * n, modes * n), jnp.float32),
             pltpu.VMEM((n, n), jnp.float32),
-            pltpu.SemaphoreType.DMA((2, 3)),
+            pltpu.SemaphoreType.DMA((3, 3)),
             pltpu.SemaphoreType.DMA((len(constant),)),
         ],
         VMEM_BYTES,

time: 223 us -> 213 us (0.955)
  the two profiles are of different devices: /device:TPU:1 before, /device:TPU:7 now
where the time goes in v4:
time: 213 us; the launch traced here: 210 us
  starting transfers between devices  103 us (48%)
  waiting for transfers between devices  50.1 us (24%)
  Pallas kernels  21.9 us (10%)
  local copies, waits for them, and re-layouts  17 us (8%)
  other arithmetic  14.7 us (7%)
  between operations  3.19 us (1%)
    ppermute x17, starting transfers between devices, peers(): lax.ppermute(v, axes, [(i, i ^ k + 1) for i in range(size)])  57.3 us
    ppermute x10, waiting for transfers between devices, to_neighbour(): return lax.ppermute(value, axes, pairs)  33.7 us
    ppermute x10, starting transfers between devices, to_neighbour(): return lax.ppermute(value, axes, pairs)  31.2 us
    pallas_call x3, Pallas kernels, call(): pl.pallas_call(kernel, in_specs=in_specs, out_specs=out_specs, scratch_sh...  19.3 us
    ppermute x17, waiting for transfers between devices, peers(): lax.ppermute(v, axes, [(i, i ^ k + 1) for i in range(size)])  16.4 us
    all_to_all x1, starting transfers between devices, shards(): lax.all_to_all(requests, ROW, split_axis=0, concat_axis=0, tiled=True)  7.5 us
    all_to_all x1, starting transfers between devices, shards(): lax.all_to_all(slots, ROW, split_axis=0, concat_axis=0, tiled=True)  7.35 us
    unnamed x24, local copies, waits for them, and re-layouts  6.46 us
  transfers between devices with their start and end apart: 29, of which 10 were waited for; matrix products, arithmetic and copies ran while one was open for 11% of the time, Pallas kernels for 6%

profile of v4, /device:TPU:7, one launch (start us, length us, event | category | flops | bytes accessed | tf_op | source)
XLA Modules:
  0.0 210.2 jit_solution(5712735241554132075)
XLA Ops:
  2.0 5.4 %collective-permute-start = (f32[2,128,512]{2,1,0:T(8,128)S(1)}, f32[2,128,512]{2,1,0:T(8,128)S(1)}, u32[]{:S(2)}, u32[]{:S(2)}) collective-permute-start(f32[2,128,512]{2,1,0:T(8,128)S(1)} %get-tuple-element.90), channel_id=1, source_target_pairs={{0,8},{8,16},{16,24},{24,32},{32,40},{40,48},{48,56},{56,64},{64,7... | collective-permute-start | bytes 1572872 | tf_op jit(solution)/shard_map/ppermute | solution.py:415
  10.1 7.5 %all-to-all-start = ((s32[16,1,3]{2,1,0:T(1,128)}), s32[16,1,3]{2,1,0:T(1,128)S(1)}, u32[]{:S(2)}, u32[]{:S(2)}) async-start(s32[16,1,3]{2,1,0:T(1,128)} %copy.20), calls=%async_computation | async-start | bytes 16384 | tf_op jit(solution)/shard_map/all_to_all | solution.py:498
  17.6 3.1 %collective-permute-done.1.refs_2_ = f32[2,128,512]{2,1,0:T(8,128)S(1)} collective-permute-done((f32[2,128,512]{2,1,0:T(8,128)S(1)}, f32[2,128,512]{2,1,0:T(8,128)S(1)}, u32[]{:S(2)}, u32[]{:S(2)}) %collective-permute-start.1) | collective-permute-done | bytes 524320 | tf_op jit(solution)/shard_map/ppermute | solution.py:415
  22.1 4.0 %collective-permute-start.2 = (f32[2,256,128]{2,1,0:T(8,128)S(1)}, f32[2,256,128]{2,1,0:T(8,128)S(1)}, u32[]{:S(2)}, u32[]{:S(2)}) collective-permute-start(f32[2,256,128]{2,1,0:T(8,128)S(1)} %pad_maximum_fusion.2), channel_id=1, source_target_pairs={{0,1},{1,2},{2,3},{3,4},{4,5},{5,6},{6,7},{8,9},{9,10},{10,11},{11... | collective-permute-start | bytes 786440 | tf_op jit(solution)/shard_map/ppermute | solution.py:415
  27.2 4.9 %collective-permute-start.4 = (f32[2,512,128]{2,1,0:T(8,128)}, f32[2,512,128]{2,1,0:T(8,128)}, u32[]{:S(2)}, u32[]{:S(2)}) collective-permute-start(f32[2,512,128]{2,1,0:T(8,128)} %get-tuple-element.89), channel_id=1, source_target_pairs={{0,1},{1,2},{2,3},{3,4},{4,5},{5,6},{6,7},{8,9},{9,10},{10,11},{11... | collective-permute-start | bytes 1572872 | tf_op jit(solution)/shard_map/ppermute | solution.py:415
  33.4 2.6 %spread.1 = bf16[16,256,256]{2,1,0:T(8,128)(2,1)} custom-call(s32[6]{0:T(128)} %bitcast.51, bf16[6,256,256]{2,1,0:T(8,128)(2,1)} %counts), custom_call_target="tpu_custom_call" | custom-call | tf_op jit(solution)/shard_map/spread/pallas_call | solution.py:46
  36.1 7.3 %all-to-all-start.1 = ((bf16[16,256,256]{2,1,0:T(8,128)(2,1)}), bf16[16,256,256]{2,1,0:T(8,128)(2,1)}, u32[]{:S(2)}, u32[]{:S(2)}) async-start(bf16[16,256,256]{2,1,0:T(8,128)(2,1)} %spread.1), calls=%async_computation.1 | async-start | bytes 4194304 | tf_op jit(solution)/shard_map/all_to_all | solution.py:492
  58.6 16.8 %collective-permute-done.5.refs_4_ = f32[2,512,128]{2,1,0:T(8,128)} collective-permute-done((f32[2,512,128]{2,1,0:T(8,128)}, f32[2,512,128]{2,1,0:T(8,128)}, u32[]{:S(2)}, u32[]{:S(2)}) %collective-permute-start.5) | collective-permute-done | bytes 524320 | tf_op jit(solution)/shard_map/ppermute | solution.py:415
  75.5 7.3 %waves.1 = (bf16[16,768,512]{2,1,0:T(8,128)(2,1)}, f32[16,2,2,256,128]{4,3,2,1,0:T(8,128)}) custom-call(s32[1]{0:T(128)} %bitcast.9.count, s32[16]{0:T(128)S(1)} %get-tuple-element.77.tops, s32[16]{0:T(128)S(1)} %get-tuple-element.76.lefts, f32[3,2,2,128,256]{4,3,2,1,0:T(8,128)} %bitcast.44, bf16[256,256]{1,0:T(8,128)(2,1)S(1)} %get-tuple-element.155.even_all, ...), custom_call_target="tpu_custom_call" | custom-call | tf_op jit(solution)/shard_map/waves/pallas_call | solution.py:331
  82.8 10.1 %frames.1 = (f32[3,2,256,256]{3,2,1,0:T(8,128)S(1)}, f32[2,784,768]{2,1,0:T(8,128)S(1)}) custom-call(s32[16]{0:T(128)} %get-tuple-element.78.order, s32[1]{0:T(128)} %bitcast.9.count, s32[16]{0:T(128)} %copy-done.3, s32[16]{0:T(128)} %copy-done.2, bf16[16,256,256]{2,1,0:T(8,128)(2,1)} %all-to-all-done.1.raw_all, ...), custom_call_target="tpu_custom_call" | custom-call | tf_op jit(solution)/shard_map/frames/pallas_call | solution.py:331
  95.2 7.3 %collective-permute-start.6 = (f32[768,256]{1,0:T(8,128)S(1)}, f32[768,256]{1,0:T(8,128)S(1)}, u32[]{:S(2)}, u32[]{:S(2)}) collective-permute-start(f32[768,256]{1,0:T(8,128)S(1)} %constant_dynamic-slice_fusion.6), channel_id=1, source_target_pairs={{0,8},{8,0},{1,9},{9,1},{2,10},{10,2},{3,11},{11,3},{4,12},{12,4},... | collective-permute-start | bytes 2359304 | tf_op jit(solution)/shard_map/ppermute | solution.py:445
  105.9 3.6 %collective-permute-start.8 = (f32[192,256]{1,0:T(8,128)S(1)}, f32[192,256]{1,0:T(8,128)S(1)}, u32[]{:S(2)}, u32[]{:S(2)}) collective-permute-start(f32[192,256]{1,0:T(8,128)S(1)} %get-tuple-element.101), channel_id=1, source_target_pairs={{0,64},{32,96},{64,0},{96,32},{1,65},{33,97},{65,1},{97,33},{2,66}... | collective-permute-start | bytes 589832 | tf_op jit(solution)/shard_map/ppermute | solution.py:445
  109.5 2.7 %convert.136 = f16[2,784,768]{2,1,0:T(8,128)(2,1)S(1)} convert(f32[2,784,768]{2,1,0:T(8,128)} %copy-done) | non-fusion elementwise | flops 1204224 | bytes 7225344 | tf_op jit(solution)/shard_map/convert.1
  112.2 6.4 %collective-permute-done.8 = f32[192,256]{1,0:T(8,128)S(1)} collective-permute-done((f32[192,256]{1,0:T(8,128)S(1)}, f32[192,256]{1,0:T(8,128)S(1)}, u32[]{:S(2)}, u32[]{:S(2)}) %collective-permute-start.8) | collective-permute-done | bytes 196640 | tf_op jit(solution)/shard_map/ppermute | solution.py:445
  118.6 2.3 %collective-permute-done.9 = f32[192,256]{1,0:T(8,128)S(1)} collective-permute-done((f32[192,256]{1,0:T(8,128)S(1)}, f32[192,256]{1,0:T(8,128)S(1)}, u32[]{:S(2)}, u32[]{:S(2)}) %collective-permute-start.9) | collective-permute-done | bytes 196640 | tf_op jit(solution)/shard_map/ppermute | solution.py:445
  122.7 4.1 %collective-permute-start.11 = (f32[48,256]{1,0:T(8,128)S(1)}, f32[48,256]{1,0:T(8,128)S(1)}, u32[]{:S(2)}, u32[]{:S(2)}) collective-permute-start(f32[48,256]{1,0:T(8,128)S(1)} %get-tuple-element.112), channel_id=1, source_target_pairs={{0,4},{2,6},{4,0},{6,2},{1,5},{3,7},{5,1},{7,3},{8,12},{10,14},{12... | collective-permute-start | bytes 147464 | tf_op jit(solution)/shard_map/ppermute | solution.py:445
  132.9 22.2 %collective-permute-start.14 = (f32[48,256]{1,0:T(8,128)S(1)}, f32[48,256]{1,0:T(8,128)S(1)}, u32[]{:S(2)}, u32[]{:S(2)}) collective-permute-start(f32[48,256]{1,0:T(8,128)S(1)} %add_add_fusion.1), channel_id=1, source_target_pairs={{0,16},{1,17},{16,0},{17,1},{2,18},{3,19},{18,2},{19,3},{4,20},{5,... | collective-permute-start | bytes 147464 | tf_op jit(solution)/shard_map/ppermute | solution.py:445
  156.5 4.9 %collective-permute-done.14 = f32[48,256]{1,0:T(8,128)S(1)} collective-permute-done((f32[48,256]{1,0:T(8,128)S(1)}, f32[48,256]{1,0:T(8,128)S(1)}, u32[]{:S(2)}, u32[]{:S(2)}) %collective-permute-start.14) | collective-permute-done | bytes 49184 | tf_op jit(solution)/shard_map/ppermute | solution.py:445
  161.5 10.5 %collective-permute-start.18 = (f32[48,256]{1,0:T(8,128)S(1)}, f32[48,256]{1,0:T(8,128)S(1)}, u32[]{:S(2)}, u32[]{:S(2)}) collective-permute-start(f32[48,256]{1,0:T(8,128)S(1)} %add_multiply_fusion), channel_id=1, source_target_pairs={{0,4},{2,6},{4,0},{6,2},{1,5},{3,7},{5,1},{7,3},{8,12},{10,14},{12... | collective-permute-start | bytes 147464 | tf_op jit(solution)/shard_map/ppermute | solution.py:445
  180.6 6.2 %collective-permute-start.24 = (f32[2,128,512]{2,1,0:T(8,128)S(1)}, f32[2,128,512]{2,1,0:T(8,128)S(1)}, u32[]{:S(2)}, u32[]{:S(2)}) collective-permute-start(f32[2,128,512]{2,1,0:T(8,128)S(1)} %get-tuple-element.95), channel_id=1, source_target_pairs={{0,8},{8,16},{16,24},{24,32},{32,40},{40,48},{48,56},{56,64},{64,7... | collective-permute-start | bytes 1572872 | tf_op jit(solution)/shard_map/ppermute | solution.py:415
  186.7 2.8 %collective-permute-start.25 = (f32[2,128,512]{2,1,0:T(8,128)S(1)}, f32[2,128,512]{2,1,0:T(8,128)S(1)}, u32[]{:S(2)}, u32[]{:S(2)}) collective-permute-start(f32[2,128,512]{2,1,0:T(8,128)S(1)} %get-tuple-element.94), channel_id=1, source_target_pairs={{8,0},{16,8},{24,16},{32,24},{40,32},{48,40},{56,48},{64,56},{72,6... | collective-permute-start | bytes 1572872 | tf_op jit(solution)/shard_map/ppermute | solution.py:415
  189.7 3.1 %collective-permute-done.24.above = f32[2,128,512]{2,1,0:T(8,128)S(1)} collective-permute-done((f32[2,128,512]{2,1,0:T(8,128)S(1)}, f32[2,128,512]{2,1,0:T(8,128)S(1)}, u32[]{:S(2)}, u32[]{:S(2)}) %collective-permute-start.24) | collective-permute-done | bytes 524320 | tf_op jit(solution)/shard_map/ppermute | solution.py:415
  192.8 10.7 %collective-permute-done.25.below = f32[2,128,512]{2,1,0:T(8,128)S(1)} collective-permute-done((f32[2,128,512]{2,1,0:T(8,128)S(1)}, f32[2,128,512]{2,1,0:T(8,128)S(1)}, u32[]{:S(2)}, u32[]{:S(2)}) %collective-permute-start.25) | collective-permute-done | bytes 524320 | tf_op jit(solution)/shard_map/ppermute | solution.py:415
  203.5 2.4 %copy-done.1 = f32[2,784,768]{2,1,0:T(8,128)S(1)} copy-done((f32[2,784,768]{2,1,0:T(8,128)S(1)}, f32[2,784,768]{2,1,0:T(8,128)}, u32[]{:S(2)}) %copy-start.1) | copy-done | bytes 4816920
  (124 shorter events, 48.8 us)
Async XLA Ops:
  2.0 15.7 %collective-permute-start = (f32[2,128,512]{2,1,0:T(8,128)S(1)}, f32[2,128,512]{2,1,0:T(8,128)S(1)}, u32[]{:S(2)}, u32[]{:S(2)}) collective-permute-start(f32[2,128,512]{2,1,0:T(8,128)S(1)} %get-tuple-element.90), channel_id=1, source_target_pairs={{0,8},{8,16},{16,24},{24,32},{32,40},{40,48},{48,56},{56,64},{64,7... | collective-permute-start | bytes 1572872 | tf_op jit(solution)/shard_map/ppermute | solution.py:415
  7.4 13.4 %collective-permute-start.1 = (f32[2,128,512]{2,1,0:T(8,128)S(1)}, f32[2,128,512]{2,1,0:T(8,128)S(1)}, u32[]{:S(2)}, u32[]{:S(2)}) collective-permute-start(f32[2,128,512]{2,1,0:T(8,128)S(1)} %get-tuple-element.91), channel_id=1, source_target_pairs={{8,0},{16,8},{24,16},{32,24},{40,32},{48,40},{56,48},{64,56},{72,6... | collective-permute-start | bytes 1572872 | tf_op jit(solution)/shard_map/ppermute | solution.py:415
  10.1 26.0 %all-to-all-start = ((s32[16,1,3]{2,1,0:T(1,128)}), s32[16,1,3]{2,1,0:T(1,128)S(1)}, u32[]{:S(2)}, u32[]{:S(2)}) async-start(s32[16,1,3]{2,1,0:T(1,128)} %copy.20), calls=%async_computation | async-start | bytes 16384 | tf_op jit(solution)/shard_map/all_to_all | solution.py:498
  20.8 12.6 %collective-permute-start.3 = (f32[2,256,128]{2,1,0:T(8,128)S(1)}, f32[2,256,128]{2,1,0:T(8,128)S(1)}, u32[]{:S(2)}, u32[]{:S(2)}) collective-permute-start(f32[2,256,128]{2,1,0:T(8,128)S(1)} %pad_maximum_fusion.3), channel_id=1, source_target_pairs={{1,0},{2,1},{3,2},{4,3},{5,4},{6,5},{7,6},{9,8},{10,9},{11,10},{12... | collective-permute-start | bytes 786440 | tf_op jit(solution)/shard_map/ppermute | solution.py:415
  22.1 11.3 %collective-permute-start.2 = (f32[2,256,128]{2,1,0:T(8,128)S(1)}, f32[2,256,128]{2,1,0:T(8,128)S(1)}, u32[]{:S(2)}, u32[]{:S(2)}) collective-permute-start(f32[2,256,128]{2,1,0:T(8,128)S(1)} %pad_maximum_fusion.2), channel_id=1, source_target_pairs={{0,1},{1,2},{2,3},{3,4},{4,5},{5,6},{6,7},{8,9},{9,10},{10,11},{11... | collective-permute-start | bytes 786440 | tf_op jit(solution)/shard_map/ppermute | solution.py:415
  27.2 31.4 %collective-permute-start.4 = (f32[2,512,128]{2,1,0:T(8,128)}, f32[2,512,128]{2,1,0:T(8,128)}, u32[]{:S(2)}, u32[]{:S(2)}) collective-permute-start(f32[2,512,128]{2,1,0:T(8,128)} %get-tuple-element.89), channel_id=1, source_target_pairs={{0,1},{1,2},{2,3},{3,4},{4,5},{5,6},{6,7},{8,9},{9,10},{10,11},{11... | collective-permute-start | bytes 1572872 | tf_op jit(solution)/shard_map/ppermute | solution.py:415
  32.1 43.3 %collective-permute-start.5 = (f32[2,512,128]{2,1,0:T(8,128)}, f32[2,512,128]{2,1,0:T(8,128)}, u32[]{:S(2)}, u32[]{:S(2)}) collective-permute-start(f32[2,512,128]{2,1,0:T(8,128)} %get-tuple-element.88), channel_id=1, source_target_pairs={{1,0},{2,1},{3,2},{4,3},{5,4},{6,5},{7,6},{9,8},{10,9},{11,10},{12... | collective-permute-start | bytes 1572872 | tf_op jit(solution)/shard_map/ppermute | solution.py:415
  36.1 46.7 %all-to-all-start.1 = ((bf16[16,256,256]{2,1,0:T(8,128)(2,1)}), bf16[16,256,256]{2,1,0:T(8,128)(2,1)}, u32[]{:S(2)}, u32[]{:S(2)}) async-start(bf16[16,256,256]{2,1,0:T(8,128)(2,1)} %spread.1), calls=%async_computation.1 | async-start | bytes 4194304 | tf_op jit(solution)/shard_map/all_to_all | solution.py:492
  95.2 9.2 %collective-permute-start.6 = (f32[768,256]{1,0:T(8,128)S(1)}, f32[768,256]{1,0:T(8,128)S(1)}, u32[]{:S(2)}, u32[]{:S(2)}) collective-permute-start(f32[768,256]{1,0:T(8,128)S(1)} %constant_dynamic-slice_fusion.6), channel_id=1, source_target_pairs={{0,8},{8,0},{1,9},{9,1},{2,10},{10,2},{3,11},{11,3},{4,12},{12,4},... | collective-permute-start | bytes 2359304 | tf_op jit(solution)/shard_map/ppermute | solution.py:445
  104.5 7.6 %collective-permute-start.7 = (f32[192,256]{1,0:T(8,128)S(1)}, f32[192,256]{1,0:T(8,128)S(1)}, u32[]{:S(2)}, u32[]{:S(2)}) collective-permute-start(f32[192,256]{1,0:T(8,128)S(1)} %get-tuple-element.99), channel_id=1, source_target_pairs={{0,32},{32,0},{64,96},{96,64},{1,33},{33,1},{65,97},{97,65},{2,34}... | collective-permute-start | bytes 589832 | tf_op jit(solution)/shard_map/ppermute | solution.py:445
  105.9 12.7 %collective-permute-start.8 = (f32[192,256]{1,0:T(8,128)S(1)}, f32[192,256]{1,0:T(8,128)S(1)}, u32[]{:S(2)}, u32[]{:S(2)}) collective-permute-start(f32[192,256]{1,0:T(8,128)S(1)} %get-tuple-element.101), channel_id=1, source_target_pairs={{0,64},{32,96},{64,0},{96,32},{1,65},{33,97},{65,1},{97,33},{2,66}... | collective-permute-start | bytes 589832 | tf_op jit(solution)/shard_map/ppermute | solution.py:445
  109.5 11.5 %collective-permute-start.9 = (f32[192,256]{1,0:T(8,128)S(1)}, f32[192,256]{1,0:T(8,128)S(1)}, u32[]{:S(2)}, u32[]{:S(2)}) collective-permute-start(f32[192,256]{1,0:T(8,128)S(1)} %get-tuple-element.100), channel_id=1, source_target_pairs={{0,96},{32,64},{64,32},{96,0},{1,97},{33,65},{65,33},{97,1},{2,98}... | collective-permute-start | bytes 589832 | tf_op jit(solution)/shard_map/ppermute | solution.py:445
  121.0 9.7 %collective-permute-start.10 = (f32[48,256]{1,0:T(8,128)S(1)}, f32[48,256]{1,0:T(8,128)S(1)}, u32[]{:S(2)}, u32[]{:S(2)}) collective-permute-start(f32[48,256]{1,0:T(8,128)S(1)} %get-tuple-element.110), channel_id=1, source_target_pairs={{0,2},{2,0},{4,6},{6,4},{1,3},{3,1},{5,7},{7,5},{8,10},{10,8},{12,... | collective-permute-start | bytes 147464 | tf_op jit(solution)/shard_map/ppermute | solution.py:445
  122.7 8.0 %collective-permute-start.11 = (f32[48,256]{1,0:T(8,128)S(1)}, f32[48,256]{1,0:T(8,128)S(1)}, u32[]{:S(2)}, u32[]{:S(2)}) collective-permute-start(f32[48,256]{1,0:T(8,128)S(1)} %get-tuple-element.112), channel_id=1, source_target_pairs={{0,4},{2,6},{4,0},{6,2},{1,5},{3,7},{5,1},{7,3},{8,12},{10,14},{12... | collective-permute-start | bytes 147464 | tf_op jit(solution)/shard_map/ppermute | solution.py:445
  127.2 34.3 %collective-permute-start.16 = (f16[2,784,128]{2,1,0:T(8,128)(2,1)S(1)}, f16[2,784,128]{2,1,0:T(8,128)(2,1)S(1)}, u32[]{:S(2)}, u32[]{:S(2)}) collective-permute-start(f16[2,784,128]{2,1,0:T(8,128)(2,1)S(1)} %get-tuple-element.87), channel_id=1, source_target_pairs={{0,1},{1,2},{2,3},{3,4},{4,5},{5,6},{6,7},{8,9},{9,10},{10,11},{11... | collective-permute-start | bytes 1204232 | tf_op jit(solution)/shard_map/ppermute | solution.py:415
  129.4 32.0 %collective-permute-start.17 = (f16[2,784,128]{2,1,0:T(8,128)(2,1)S(1)}, f16[2,784,128]{2,1,0:T(8,128)(2,1)S(1)}, u32[]{:S(2)}, u32[]{:S(2)}) collective-permute-start(f16[2,784,128]{2,1,0:T(8,128)(2,1)S(1)} %get-tuple-element.86), channel_id=1, source_target_pairs={{1,0},{2,1},{3,2},{4,3},{5,4},{6,5},{7,6},{9,8},{10,9},{11,10},{12... | collective-permute-start | bytes 1204232 | tf_op jit(solution)/shard_map/ppermute | solution.py:415
  131.0 25.5 %collective-permute-start.13 = (f32[48,256]{1,0:T(8,128)S(1)}, f32[48,256]{1,0:T(8,128)S(1)}, u32[]{:S(2)}, u32[]{:S(2)}) collective-permute-start(f32[48,256]{1,0:T(8,128)S(1)} %add_add_fusion.1), channel_id=1, source_target_pairs={{0,1},{1,0},{16,17},{17,16},{2,3},{3,2},{18,19},{19,18},{4,5},{5,4... | collective-permute-start | bytes 147464 | tf_op jit(solution)/shard_map/ppermute | solution.py:445
  132.9 28.5 %collective-permute-start.14 = (f32[48,256]{1,0:T(8,128)S(1)}, f32[48,256]{1,0:T(8,128)S(1)}, u32[]{:S(2)}, u32[]{:S(2)}) collective-permute-start(f32[48,256]{1,0:T(8,128)S(1)} %add_add_fusion.1), channel_id=1, source_target_pairs={{0,16},{1,17},{16,0},{17,1},{2,18},{3,19},{18,2},{19,3},{4,20},{5,... | collective-permute-start | bytes 147464 | tf_op jit(solution)/shard_map/ppermute | solution.py:445
  161.5 15.1 %collective-permute-start.18 = (f32[48,256]{1,0:T(8,128)S(1)}, f32[48,256]{1,0:T(8,128)S(1)}, u32[]{:S(2)}, u32[]{:S(2)}) collective-permute-start(f32[48,256]{1,0:T(8,128)S(1)} %add_multiply_fusion), channel_id=1, source_target_pairs={{0,4},{2,6},{4,0},{6,2},{1,5},{3,7},{5,1},{7,3},{8,12},{10,14},{12... | collective-permute-start | bytes 147464 | tf_op jit(solution)/shard_map/ppermute | solution.py:445
  177.2 12.3 %collective-permute-start.21 = (f32[192,256]{1,0:T(8,128)S(1)}, f32[192,256]{1,0:T(8,128)S(1)}, u32[]{:S(2)}, u32[]{:S(2)}) collective-permute-start(f32[192,256]{1,0:T(8,128)S(1)} %pad_maximum_fusion.4), channel_id=1, source_target_pairs={{0,64},{32,96},{64,0},{96,32},{1,65},{33,97},{65,1},{97,33},{2,66}... | collective-permute-start | bytes 589832 | tf_op jit(solution)/shard_map/ppermute | solution.py:445
  177.9 11.6 %collective-permute-start.22 = (f32[192,256]{1,0:T(8,128)S(1)}, f32[192,256]{1,0:T(8,128)S(1)}, u32[]{:S(2)}, u32[]{:S(2)}) collective-permute-start(f32[192,256]{1,0:T(8,128)S(1)} %pad_maximum_fusion.4), channel_id=1, source_target_pairs={{0,32},{32,0},{64,96},{96,64},{1,33},{33,1},{65,97},{97,65},{2,34}... | collective-permute-start | bytes 589832 | tf_op jit(solution)/shard_map/ppermute | solution.py:445
  179.9 9.7 %collective-permute-start.23 = (f32[192,256]{1,0:T(8,128)S(1)}, f32[192,256]{1,0:T(8,128)S(1)}, u32[]{:S(2)}, u32[]{:S(2)}) collective-permute-start(f32[192,256]{1,0:T(8,128)S(1)} %pad_maximum_fusion.4), channel_id=1, source_target_pairs={{0,96},{32,64},{64,32},{96,0},{1,97},{33,65},{65,33},{97,1},{2,98}... | collective-permute-start | bytes 589832 | tf_op jit(solution)/shard_map/ppermute | solution.py:445
  180.6 12.3 %collective-permute-start.24 = (f32[2,128,512]{2,1,0:T(8,128)S(1)}, f32[2,128,512]{2,1,0:T(8,128)S(1)}, u32[]{:S(2)}, u32[]{:S(2)}) collective-permute-start(f32[2,128,512]{2,1,0:T(8,128)S(1)} %get-tuple-element.95), channel_id=1, source_target_pairs={{0,8},{8,16},{16,24},{24,32},{32,40},{40,48},{48,56},{56,64},{64,7... | collective-permute-start | bytes 1572872 | tf_op jit(solution)/shard_map/ppermute | solution.py:415
  186.7 16.8 %collective-permute-start.25 = (f32[2,128,512]{2,1,0:T(8,128)S(1)}, f32[2,128,512]{2,1,0:T(8,128)S(1)}, u32[]{:S(2)}, u32[]{:S(2)}) collective-permute-start(f32[2,128,512]{2,1,0:T(8,128)S(1)} %get-tuple-element.94), channel_id=1, source_target_pairs={{8,0},{16,8},{24,16},{32,24},{40,32},{48,40},{56,48},{64,56},{72,6... | collective-permute-start | bytes 1572872 | tf_op jit(solution)/shard_map/ppermute | solution.py:415
  (16 other events, 121.8 us)
